TPU v7x, 256 devices: a whole 4x4x8 slice. The times are simulated.
256 devices in a mesh: row: 32 (over z, y_hi, core), col: 8 (over x, y_lo).
Axes of the slice: x: 4, y: 4 (y_hi: 2, y_lo: 2; y = y_hi * 2 + y_lo), z: 8, core: 2. Of those that a mesh axis runs over, the one named last changes fastest.
Arguments:
- matrix: float32 [32, 8, 64, 4, 32, 128], P(None, 'col', None, None, 'row'), may hold values from -6 to 128, as said below
- column_weight: float32 [4, 32, 128], P(None, 'row'), may hold values from -0.046875 to 0.046875
- row_weight: float32 [32, 8, 64], P(None, 'col'), may hold values from -0.046875 to 0.046875
Outputs:
- factored: float32 [32, 8, 64, 4, 32, 128], P(None, 'col', None, None, 'row')
- row_checks: float32 [32, 8, 64], P(None, 'col')
- column_checks: float32 [4, 32, 128], P(None, 'row')
Inputs may be any that keep to these rules, and one draw needn't show every extreme that they name: `matrix`: the diagonal entries lie between 64 and 128; every other entry has magnitude at most 6.
All inputs are finite; a program needn't handle non-finite values.
Results may differ from a plain program's by a relative error of at most 0.0003.
Values sent between devices are 32-bit elements; how exact they have to be, the bound alone decides.
A program may use at most 64 MiB of HBM per device.

v0:
```python
import jax
import jax.numpy as jnp
from jax import lax
from jax.sharding import PartitionSpec as P

highest = lax.Precision.HIGHEST


def spread(x, axis, root):
    mine = lax.axis_index(axis) == root
    return lax.psum(jnp.where(mine, x, jnp.zeros_like(x)), axis)


def product(left, right):
    return jnp.dot(left, right, precision=highest, preferred_element_type=jnp.float32)


def unit_inverse(nilpotent, identity, side_len):
    result = identity - nilpotent
    power = product(nilpotent, nilpotent)
    reach = 2
    while reach < side_len:
        result = product(result, identity + power)
        power = product(power, power)
        reach = reach * 2
    return result


def factor_small(square):
    side_len = square.shape[0]
    positions = jnp.arange(side_len)
    packed = square
    for pivot_at in range(side_len):
        column = packed[:, pivot_at]
        across = packed[pivot_at, :]
        below = positions > pivot_at
        ratios = jnp.where(below, column / packed[pivot_at, pivot_at], 0.0)
        beyond = below[:, None] & below[None, :]
        packed = packed - jnp.where(beyond, ratios[:, None] * across[None, :], 0.0)
        packed = packed.at[:, pivot_at].set(jnp.where(below, ratios, column))
    identity = jnp.eye(side_len, dtype=square.dtype)
    strict_low = jnp.where(positions[:, None] > positions[None, :], packed, 0.0)
    lower = strict_low + identity
    upper = jnp.where(positions[:, None] <= positions[None, :], packed, 0.0)
    lower_inv = unit_inverse(strict_low, identity, side_len)
    diag_vals = jnp.diagonal(packed)
    strict_up = jnp.where(positions[:, None] < positions[None, :], packed / diag_vals[:, None], 0.0)
    upper_inv = unit_inverse(strict_up, identity, side_len) / diag_vals[None, :]
    return (lower, upper, lower_inv, upper_inv)


def factor_parts(square):
    side_len = square.shape[0]
    if side_len <= 16:
        return factor_small(square)
    half = side_len // 2
    lower_a, upper_a, linv_a, uinv_a = factor_parts(square[:half, :half])
    left_low = product(square[half:, :half], uinv_a)
    right_up = product(linv_a, square[:half, half:])
    schur = square[half:, half:] - product(left_low, right_up)
    lower_b, upper_b, linv_b, uinv_b = factor_parts(schur)
    zeros = jnp.zeros((half, side_len - half), square.dtype)
    lower = jnp.block([[lower_a, zeros], [left_low, lower_b]])
    upper = jnp.block([[upper_a, right_up], [zeros.T, upper_b]])
    linv_off = -product(linv_b, product(left_low, linv_a))
    uinv_off = -product(uinv_a, product(right_up, uinv_b))
    lower_inv = jnp.block([[linv_a, zeros], [linv_off, linv_b]])
    upper_inv = jnp.block([[uinv_a, uinv_off], [zeros.T, uinv_b]])
    return (lower, upper, lower_inv, upper_inv)


def factor_block(square):
    lower, upper, lower_inv, upper_inv = factor_parts(square)
    side_len = square.shape[0]
    positions = jnp.arange(side_len)
    packed = jnp.where(positions[:, None] > positions[None, :], lower, upper)
    return (packed, lower_inv, upper_inv)


def per_device(matrix, column_weight, row_weight):
    panel_width = matrix.shape[2]
    block_width = matrix.shape[5]
    row_count = matrix.shape[0] * matrix.shape[1] * matrix.shape[2]
    col_count = matrix.shape[3] * matrix.shape[4] * matrix.shape[5]
    entries = matrix.reshape(row_count, col_count)
    weights_across = column_weight.reshape(col_count)
    weights_down = row_weight.reshape(row_count)
    down_count = lax.axis_size("col")
    across_count = lax.axis_size("row")
    mine_down = lax.axis_index("col")
    mine_across = lax.axis_index("row")
    local_rows = jnp.arange(row_count)
    local_cols = jnp.arange(col_count)
    global_rows = (
        local_rows // panel_width * down_count + mine_down
    ) * panel_width + local_rows % panel_width
    global_cols = (
        local_cols // block_width * across_count + mine_across
    ) * block_width + local_cols % block_width
    row_checks = lax.psum(product(entries, weights_across), "row")
    column_checks = lax.psum(product(weights_down, entries), "col")
    for step_index in range(2):
        first_col = step_index * panel_width
        end_col = first_col + panel_width
        panel_now, checks_top = (
            spread(entries[:, first_col:end_col], "row", 0),
            spread(column_checks[first_col:end_col], "row", 0),
        )
        pivot_entries = entries
        pivot_row_checks = row_checks
        pivot_column_checks = column_checks
        strip_now = panel_now[:panel_width]
        pivot_first_col = step_index * panel_width
        pivot_end_col = pivot_first_col + panel_width
        pivot_down = mine_down == step_index
        pivot_across = mine_across == 0
        row_tail = global_rows >= pivot_end_col
        col_tail = global_cols >= pivot_end_col
        top_rows = pivot_entries[:panel_width]
        top_checks = pivot_row_checks[:panel_width]
        top_rows, top_checks, strip_now = (
            spread(top_rows, "col", step_index),
            spread(top_checks, "col", step_index),
            spread(strip_now, "col", step_index),
        )
        packed, lower_inv, upper_inv = factor_block(strip_now[:, :panel_width])
        left_part = product(panel_now, upper_inv)
        right_part = product(lower_inv, top_rows)
        check_down = product(lower_inv, top_checks)
        check_across = product(checks_top, upper_inv)
        left_masked = jnp.where(row_tail[:, None], left_part, 0.0)
        right_masked = jnp.where(col_tail[None, :], right_part, 0.0)
        pivot_entries = pivot_entries - product(left_masked, right_masked)
        pivot_row_checks = jnp.where(
            row_tail, pivot_row_checks - product(left_part, check_down), pivot_row_checks
        )
        pivot_column_checks = jnp.where(
            col_tail, pivot_column_checks - product(check_across, right_part), pivot_column_checks
        )
        head_rows = pivot_entries[:panel_width]
        head_rows = jnp.where(pivot_down & col_tail[None, :], right_part, head_rows)
        pivot_entries = pivot_entries.at[:panel_width].set(head_rows)
        pivot_row_checks = pivot_row_checks.at[:panel_width].set(
            jnp.where(pivot_down, check_down, pivot_row_checks[:panel_width])
        )
        new_panel = jnp.where(row_tail[:, None], left_part, panel_now)
        new_panel = new_panel.at[:panel_width].set(
            jnp.where(pivot_down, packed, new_panel[:panel_width])
        )
        old_cols = pivot_entries[:, pivot_first_col:pivot_end_col]
        pivot_entries = pivot_entries.at[:, pivot_first_col:pivot_end_col].set(
            jnp.where(pivot_across, new_panel, old_cols)
        )
        pivot_column_checks = pivot_column_checks.at[pivot_first_col:pivot_end_col].set(
            jnp.where(
                pivot_across, check_across, pivot_column_checks[pivot_first_col:pivot_end_col]
            )
        )
        entries, row_checks, column_checks = (pivot_entries, pivot_row_checks, pivot_column_checks)
    return (
        entries.reshape(matrix.shape),
        row_checks.reshape(row_weight.shape),
        column_checks.reshape(column_weight.shape),
    )


def solution(mesh):
    return jax.shard_map(
        per_device,
        mesh=mesh,
        in_specs=(
            P(None, "col", None, None, "row", None),
            P(None, "row", None),
            P(None, "col", None),
        ),
        out_specs=(
            P(None, "col", None, None, "row", None),
            P(None, "col", None),
            P(None, "row", None),
        ),
        check_vma=False,
    )
```

profile of v0, /device:TPU:135, one launch (start us, length us, event | category | flops | bytes accessed | tf_op | source)
XLA Modules:
  0.0 1204.1 jit_solution(6923936249764032224)
XLA Ops:
  7.2 4.6 copy.42
  11.9 2.3 slice_select_fusion.1
  29.3 4.4 fusion.508
  33.7 3.6 fusion.307
  37.4 246.1 %all-reduce.32.cloned.1.call-done = f32[2048,64]{1,0:T(8,128)} async-done(((f32[2048,64]{1,0:T(8,128)}), f32[2048,64]{1,0:T(8,128)}) %all-reduce.32.cloned.1.call-update) | async-done | bytes 524304 | tf_op jit(solution)/shard_map/psum | solution.py:11
  284.2 25.3 %all-reduce.26 = (f32[64,64]{1,0:T(8,128)S(1)}, f32[512]{0:T(512)S(1)}) all-reduce(f32[64,64]{1,0:T(8,128)S(1)} %slice_select_fusion.8, f32[512]{0:T(512)S(1)} %bitcast.643), channel_id=1, replica_groups=mesh['row'=32,'col'=8] {'col'}, use_global_device_ids=true, to_apply=%region_1.2 | all-reduce | flops 4608 | bytes 36864 | tf_op jit(solution)/shard_map/psum | solution.py:11
  340.1 1.4 slice_select_fusion.118
  388.6 1.4 slice_select_fusion.103
  437.6 1.4 slice_select_fusion.88
  485.9 1.4 slice_select_fusion.73
  504.0 74.1 %psum.94 = f32[64]{0:T(128)S(1)} all-reduce(f32[64]{0:T(128)S(1)} %broadcast_select_fusion.6), channel_id=1, replica_groups=mesh['row'=32,'col'=8] {'row'}, use_global_device_ids=true, to_apply=%region_27.28 | all-reduce | flops 64 | bytes 512 | tf_op jit(solution)/shard_map/psum | solution.py:11
  580.6 67.0 %all-reduce.24 = (f32[2048]{0:T(1024)S(1)}, f32[64]{0:T(128)S(1)}) all-reduce(f32[2048]{0:T(1024)S(1)} %bitcast.642, f32[64]{0:T(128)S(1)} %broadcast_select_fusion.4), channel_id=1, replica_groups=mesh['row'=32,'col'=8] {'row'}, use_global_device_ids=true, to_apply=%region_23.24 | all-reduce | flops 2112 | bytes 16896 | tf_op jit(solution)/shard_map/psum | solution.py:100
  647.6 12.2 %psum.91 = f32[64]{0:T(128)S(1)} all-reduce(f32[64]{0:T(128)S(1)} %broadcast_select_fusion.10), channel_id=1, replica_groups=mesh['row'=32,'col'=8] {'col'}, use_global_device_ids=true, to_apply=%region_24.25 | all-reduce | flops 64 | bytes 512 | tf_op jit(solution)/shard_map/psum | solution.py:11
  662.3 5.9 convolution_subtract_fusion.1
  668.7 1.6 copy-done.2
  671.1 5.8 scatter.570
  677.0 2.6 slice_select_fusion
  679.7 1.6 slice_select_fusion.3
  681.3 269.9 %all-reduce.36.cloned.1.call-done = f32[2048,64]{1,0:T(8,128)} async-done(((f32[2048,64]{1,0:T(8,128)}), f32[2048,64]{1,0:T(8,128)}) %all-reduce.36.cloned.1.call-update) | async-done | bytes 524304 | tf_op jit(solution)/shard_map/psum | solution.py:11
  952.0 24.9 %all-reduce.25 = (f32[64,64]{1,0:T(8,128)S(1)}, f32[64]{0:T(128)S(1)}) all-reduce(f32[64,64]{1,0:T(8,128)S(1)} %slice_select_fusion.6, f32[64]{0:T(128)S(1)} %get-tuple-element.1671), channel_id=1, replica_groups=mesh['row'=32,'col'=8] {'col'}, use_global_device_ids=true, to_apply=%region_20.21 | all-reduce | flops 4160 | bytes 33280 | tf_op jit(solution)/shard_map/psum | solution.py:11
  1177.3 5.3 convolution_subtract_fusion
  1183.1 1.5 copy-done.3
  1185.6 6.6 scatter.681
  1192.2 5.2 reshape.3590
  (1026 shorter events, 412.6 us)
Async XLA Ops:
  7.2 26.5 %copy-start = (f32[4,1,128]{2,1,0:T(1,128)S(1)}, f32[4,1,128]{2,1,0:T(1,128)}, u32[]{:S(2)}) copy-start(f32[4,1,128]{2,1,0:T(1,128)} %param.280) | copy-start | bytes 6148
  7.2 276.3 %all-reduce.32.cloned.1.call-start = ((), (), s32[]{:S(2)}) async-start(), calls=%async_computation | async-start | bytes 2097152 | tf_op jit(solution)/shard_map/psum | solution.py:11
  7.2 21.3 %copy-start.6 = (f32[32,1,64]{2,1,0:T(1,128)S(1)}, f32[32,1,64]{2,1,0:T(1,128)}, u32[]{:S(2)}) copy-start(f32[32,1,64]{2,1,0:T(1,128)} %param.281) | copy-start | bytes 24580
  14.2 564.9 %all-reduce.34.cloned.1.call-start = ((), (), s32[]{:S(2)}) async-start(), calls=%async_computation.1 | async-start | bytes 262144 | tf_op jit(solution)/shard_map/psum | solution.py:11
  16.3 934.9 %all-reduce.36.cloned.1.call-start = ((), (), s32[]{:S(2)}) async-start(), calls=%async_computation.2 | async-start | bytes 2097152 | tf_op jit(solution)/shard_map/psum | solution.py:11
  29.3 4.4 copy-start.1
  356.1 304.0 %copy-start.4 = (f32[2048,64]{1,0:T(8,128)S(1)}, f32[2048,64]{1,0:T(8,128)}, u32[]{:S(2)}) copy-start(f32[2048,64]{1,0:T(8,128)} %all-reduce.32.cloned.1.call-done) | copy-start | bytes 1572868
  668.3 2.0 copy-start.2
  679.6 492.9 %all-reduce.38.cloned.1.call-start = ((), (), s32[]{:S(2)}) async-start(), calls=%async_computation.3 | async-start | bytes 262144 | tf_op jit(solution)/shard_map/psum | solution.py:11
  1023.6 150.7 %copy-start.5 = (f32[2048,64]{1,0:T(8,128)S(1)}, f32[2048,64]{1,0:T(8,128)}, u32[]{:S(2)}) copy-start(f32[2048,64]{1,0:T(8,128)} %all-reduce.36.cloned.1.call-done) | copy-start | bytes 1572868
  1174.1 8.5 copy-start.7
  1182.6 1.9 copy-start.3
Sparse Core Ops, SparseCore 0:
  14.4 269.0 all-reduce.31
  286.8 73.2 all-reduce.33
  679.7 271.4 all-reduce.35
  953.8 73.4 all-reduce.37
where the time goes:
time: 1230 us; the launch traced here: 1200 us
  waiting for transfers between devices  516 us (42%)
  other arithmetic  301 us (24%)
  blocking collectives  203 us (17%)
  local copies, waits for them, and re-layouts  121 us (10%)
  matrix products  47.2 us (4%)
  between operations  15.3 us (1%)
    psum x4, waiting for transfers between devices, spread(): return lax.psum(jnp.where(mine, x, jnp.zeros_like(x)), axis)  516 us
    another operation x139, other arithmetic  175 us
    psum x4, blocking collectives, spread(): return lax.psum(jnp.where(mine, x, jnp.zeros_like(x)), axis)  136 us
    select_n x120, other arithmetic, factor_small(): ratios = jnp.where(below, column / packed[pivot_at, pivot_at], 0.0)  97.7 us
    slice x128, local copies, waits for them, and re-layouts, factor_small(): ratios = jnp.where(below, column / packed[pivot_at, pivot_at], 0.0)  75.2 us
    psum x1, blocking collectives, per_device(): row_checks = lax.psum(product(entries, weights_across), 'row')  67 us
    dot_general x154, matrix products, product(): jnp.dot(left, right, precision=highest, preferred_element_type=jnp.float32)  47.2 us
  transfers between devices with their start and end apart: 4, of which 2 were waited for; matrix products, arithmetic and copies ran while one was open for 35% of the time, Pallas kernels for 0%

commit v1 on v0

v1 whole, which is shorter than its diff:
```python
import jax
import jax.numpy as jnp
from jax import lax
from jax.experimental import pallas as pl
from jax.experimental.pallas import tpu as pltpu
from jax.sharding import PartitionSpec as P

MESH = pl.DeviceIdType.MESH
highest = lax.Precision.HIGHEST
F32 = jnp.float32
BF16 = jnp.bfloat16
NZ = 8
CH = 8
STEPS = 8


def spread_lane(x, i):
    return jnp.broadcast_to(x[:, i : i + 1], (8, 128))


def eliminate(g_ref, inv_ref, rows_ref, low_ref):
    lane = lax.broadcasted_iota(jnp.int32, (8, 128), 1)
    sub = lax.broadcasted_iota(jnp.int32, (8, 128), 0)
    low_ref[...] = jnp.zeros((128, 128), F32)

    def strip(s, vs):
        vs = list(vs)
        cols = [jnp.zeros((8, 128), F32)] * 16
        kept = jnp.zeros((8, 128), F32)
        for i in range(8):
            row = jnp.broadcast_to(vs[0][i : i + 1, :], (8, 128))
            here = lane == i
            recip = 1.0 / spread_lane(row, i)
            scaled = jnp.where(here, recip, row * recip)
            kept = jnp.where(sub == i, row, kept)
            for j in range(16):
                new = jnp.where(here, 0.0, vs[j]) - spread_lane(vs[j], i) * scaled
                cols[j] = jnp.where(here, -new, cols[j])
                if j == 0:
                    new = jnp.where(sub == i, scaled, new)
                vs[j] = new
        turn = s * 8
        rows_ref[pl.ds(pl.multiple_of(turn, 8), 8), :] = pltpu.roll(kept, turn, 1)
        for j in range(16):
            at = pl.multiple_of(lax.rem(s + j, 16) * 8, 8)
            low_ref[pl.ds(at, 8), :] += pltpu.roll(
                jnp.where(lane < 8, cols[j], 0.0), turn, 1
            )
        return tuple(pltpu.roll(x, 120, 1) for x in vs[1:] + vs[:1])

    out = lax.fori_loop(
        0, 16, strip, tuple(g_ref[8 * j : 8 * j + 8, :] for j in range(16))
    )
    for j in range(16):
        inv_ref[8 * j : 8 * j + 8, :] = out[j]


def exchange(
    a_hbm, w_hbm, v_hbm,
    p_ref, t_ref, inv_ref, rows_ref, low_ref, r_ref, rk_ref, c_ref,
    a_ref, w_ref, v_ref, rq_ref, rz_ref, rs_ref, cz_ref,
    load_sem, t_send, t_recv, own_recv, sib_recv, y_recv, rel_recv,
    dn_send, dn2_send, sib_send, y_send, rel_send, root_send,
    rq_send, rq_recv, rz_send, rz_recv, rg_send, rg_recv, rk_send, rk_recv,
    c_send, c_recv, i_send, i_recv, l_send, l_recv,
):
    me = lax.axis_index("row")
    col = lax.axis_index("col")
    z = me // 4
    q = lax.rem(me, 4)
    is_root = me == 0
    heads = col < 2

    def at_row(r):
        return dict(row=r, col=col)

    z_peers = [at_row(lax.rem(z + d, NZ) * 4 + q) for d in range(1, NZ)]
    q_peers = [at_row(z * 4 + lax.rem(q + d, 4)) for d in range(1, 4)]
    c_peers = [dict(row=me, col=lax.rem(col + d, 8)) for d in range(1, 8)]
    sib = at_row(z * 4 + (q + 1 - 2 * lax.rem(q, 2)))
    opp = at_row(z * 4 + lax.rem(q + 2, 4))

    loads = [
        pltpu.make_async_copy(a_hbm.at[:, b, :], a_ref.at[b], load_sem.at[b])
        for b in range(4)
    ]
    loads.append(pltpu.make_async_copy(w_hbm, w_ref, load_sem.at[4]))
    loads.append(pltpu.make_async_copy(v_hbm, v_ref, load_sem.at[5]))
    for x in loads:
        x.start()
    barrier = pltpu.get_barrier_semaphore()
    for x in z_peers + q_peers + c_peers:
        pl.semaphore_signal(barrier, inc=1, device_id=x, device_id_type=MESH)
    for x in loads:
        x.wait()

    def sums(t, acc):
        at = pl.multiple_of(t * 64, 64)
        v = jnp.broadcast_to(v_ref[pl.ds(t, 1), :], (128, 64)).T
        across = jnp.zeros((64, 128), F32)
        out = []
        for b in range(4):
            block = a_ref[b, pl.ds(at, 64), :]
            across = across + block * w_ref[b : b + 1, :]
            out.append(acc[b] + (block * v).reshape(8, 8, 128).sum(0))
        r_ref[pl.ds(t, 1), 0:64] = jnp.sum(across.T, axis=0, keepdims=True)
        return tuple(out)

    r_ref[...] = jnp.zeros((32, 128), F32)
    acc = lax.fori_loop(0, 32, sums, tuple(jnp.zeros((8, 128), F32) for _ in range(4)))
    for b in range(4):
        c_ref[b : b + 1, :] = jnp.sum(acc[b], axis=0, keepdims=True)
    c_ref[4:8, :] = jnp.zeros((4, 128), F32)

    @pl.when(is_root)
    def _():
        p_ref[...] = a_ref[0]

    pl.semaphore_wait(barrier, 17)

    @pl.when(heads)
    def _():
        mine = pl.ds(pl.multiple_of(col * 64, 64), 64)
        t_ref[:, mine, :] = a_ref[:, 0:64, :]

    def t_copy(part, i, src):
        blocks = pl.ds(0, 1) if part == 0 else pl.ds(1, 3)
        mine = pl.ds(pl.multiple_of(src * 64, 64), 64)
        return pltpu.make_async_remote_copy(
            t_ref.at[blocks, mine, :], t_ref.at[blocks, mine, :],
            t_send.at[part * 7 + i], t_recv.at[part * 2 + src],
            device_id=c_peers[i], device_id_type=MESH,
        )

    @pl.when(heads)
    def _():
        for i in range(7):
            t_copy(0, i, col).start()

    cz_ref[pl.ds(col, 1)] = c_ref[...][None]

    def c_copy(i):
        return pltpu.make_async_remote_copy(
            cz_ref.at[col], cz_ref.at[col], c_send.at[i], c_recv.at[i],
            device_id=c_peers[i], device_id_type=MESH,
        )

    for i in range(7):
        c_copy(i).start()

    def rq_copy(i):
        to = lax.rem(q + i + 1, 4)
        return pltpu.make_async_remote_copy(
            r_ref.at[pl.ds(pl.multiple_of(to * 8, 8), 8)], rq_ref.at[i],
            rq_send.at[i], rq_recv.at[i],
            device_id=q_peers[i], device_id_type=MESH,
        )

    for i in range(3):
        rq_copy(i).start()

    def piece(n, k):
        return pl.ds(pl.multiple_of(n * (CH * 64) + k * 64, 64), 64)

    def p_copy(n, k, send, recv, to):
        return pltpu.make_async_remote_copy(
            p_ref.at[piece(n, k)], p_ref.at[piece(n, k)],
            send.at[k], recv.at[k], device_id=to, device_id_type=MESH,
        )

    up_side = z < 4
    has_dn = jnp.logical_and(z != 4, z != 5)
    dn_to = at_row(jnp.where(up_side, z + 1, jnp.where(has_dn, z - 1, z + 1)) * 4 + q)
    dn2_to = at_row(7 * 4 + q)
    at_zero = z == 0
    to_sib = jnp.logical_not(jnp.logical_and(at_zero, q == 1))
    to_opp = jnp.logical_not(jnp.logical_and(at_zero, q == 2))
    sib_n = q + 1 - 2 * lax.rem(q, 2)
    opp_n = lax.rem(q + 2, 4)

    def pass_own(k):
        @pl.when(has_dn)
        def _():
            p_copy(q, k, dn_send, own_recv, dn_to).start()

        @pl.when(at_zero)
        def _():
            p_copy(q, k, dn2_send, own_recv, dn2_to).start()

        @pl.when(to_opp)
        def _():
            p_copy(q, k, y_send, y_recv, opp).start()

        @pl.when(to_sib)
        def _():
            p_copy(q, k, sib_send, sib_recv, sib).start()

    def pass_opp(k):
        @pl.when(to_sib)
        def _():
            p_copy(opp_n, k, rel_send, rel_recv, sib).start()

    def root_copy(n, k):
        return pltpu.make_async_remote_copy(
            p_ref.at[piece(n, k)], p_ref.at[piece(n, k)],
            root_send.at[(n - 1) * CH + k], own_recv.at[k],
            device_id=at_row(n), device_id_type=MESH,
        )

    @pl.when(is_root)
    def _():
        def body(k, _):
            for n in (2, 3, 1):
                root_copy(n, k).start()
            pass_own(k)
            pass_opp(k)
            return 0

        lax.fori_loop(0, CH, body, 0)

    @pl.when(heads)
    def _():
        for i in range(7):
            t_copy(1, i, col).start()

    for i in range(3):
        rq_copy(i).wait()
    quarter = pl.ds(pl.multiple_of(q * 8, 8), 8)
    total = r_ref[quarter, :]
    by_source = [rq_ref[i] for i in range(3)]
    total = total + by_source[0] + by_source[1] + by_source[2]
    rz_ref[pl.ds(z, 1)] = total[None]

    def rz_copy(i):
        return pltpu.make_async_remote_copy(
            rz_ref.at[z], rz_ref.at[z], rz_send.at[i], rz_recv.at[i],
            device_id=z_peers[i], device_id_type=MESH,
        )

    def rz_arrival(i):
        return pltpu.make_async_remote_copy(
            rz_ref.at[z], rz_ref.at[lax.rem(z + NZ - 1 - i, NZ)], rz_send.at[i], rz_recv.at[i],
            device_id=z_peers[i], device_id_type=MESH,
        )

    for i in range(7):
        rz_copy(i).start()

    def take_own(k, _):
        p_copy(q, k, dn_send, own_recv, dn_to).wait_recv()
        pass_own(k)
        return 0

    def take_opp(k, _):
        p_copy(opp_n, k, y_send, y_recv, opp).wait_recv()
        pass_opp(k)
        return 0

    not_root = jnp.logical_not(is_root)

    @pl.when(not_root)
    def _():
        lax.fori_loop(0, 4, take_own, 0)

    @pl.when(is_root)
    def _():
        for s in range(2):
            @pl.when(col != s)
            def _():
                t_copy(0, 0, s).wait_recv()
        eliminate(t_ref.at[0], inv_ref.at[pl.ds(0, 128)], rows_ref, low_ref)

    def rg_copy(i):
        return pltpu.make_async_remote_copy(
            rs_ref.at[quarter], rs_ref.at[quarter], rg_send.at[i], rg_recv.at[i],
            device_id=q_peers[i], device_id_type=MESH,
        )

    def rg_arrival(i):
        theirs = pl.ds(pl.multiple_of(lax.rem(q + 3 - i, 4) * 8, 8), 8)
        return pltpu.make_async_remote_copy(
            rs_ref.at[theirs], rs_ref.at[theirs], rg_send.at[i], rg_recv.at[i],
            device_id=q_peers[i], device_id_type=MESH,
        )

    for i in range(7):
        c_copy(i).wait_recv()
    over = cz_ref[0]
    for i in range(1, 8):
        over = over + cz_ref[i]
    c_ref[...] = over

    def i_copy(i, to):
        return pltpu.make_async_remote_copy(
            inv_ref, inv_ref, i_send.at[i], i_recv.at[0], device_id=to, device_id_type=MESH
        )

    def l_copy(i, to):
        return pltpu.make_async_remote_copy(
            rows_ref, rows_ref, l_send.at[i], l_recv.at[0], device_id=to, device_id_type=MESH
        )

    def inv_to(i, to):
        i_copy(i, to).start()

        @pl.when(heads)
        def _():
            l_copy(i, to).start()

    def inv_wait(i, to):
        i_copy(i, to).wait_send()

        @pl.when(heads)
        def _():
            l_copy(i, to).wait_send()

    @pl.when(is_root)
    def _():
        inv_ref[128:136, :] = over
        for i in (2, 3, 1, 4, 0, 5, 6):
            inv_to(i, z_peers[i])
        inv_to(7, opp)
        inv_to(8, sib)

    for i in range(7):
        rz_arrival(i).wait_recv()
    whole = rz_ref[0]
    for i in range(1, 8):
        whole = whole + rz_ref[i]
    rs_ref[quarter, :] = whole
    for i in range(3):
        rg_copy(i).start()

    @pl.when(not_root)
    def _():
        lax.fori_loop(4, CH, take_own, 0)
        lax.fori_loop(0, CH, take_opp, 0)

    for i in range(3):
        rg_arrival(i).wait_recv()

    def rk_copy(i):
        return pltpu.make_async_remote_copy(
            rs_ref.at[pl.ds(0, 8)], rk_ref.at[col], rk_send.at[i], rk_recv.at[col],
            device_id=c_peers[i], device_id_type=MESH,
        )

    @pl.when(heads)
    def _():
        rk_ref[pl.ds(col, 1)] = rs_ref[0:8, :][None]
        for i in range(7):
            rk_copy(i).start()

    @pl.when(not_root)
    def _():
        i_copy(0, sib).wait_recv()

        @pl.when(heads)
        def _():
            l_copy(0, sib).wait_recv()

        @pl.when(jnp.logical_and(q == 0, z > 0))
        def _():
            inv_to(7, opp)

        @pl.when(jnp.logical_or(q == 2, jnp.logical_and(q == 0, z > 0)))
        def _():
            inv_to(8, sib)

    for s in range(2):
        @pl.when(col != s)
        def _():
            @pl.when(not_root)
            def _():
                t_copy(0, 0, s).wait_recv()

            t_copy(1, 0, s).wait_recv()
            pltpu.make_async_remote_copy(
                rs_ref.at[pl.ds(0, 8)], rk_ref.at[s], rk_send.at[0], rk_recv.at[s],
                device_id=c_peers[0], device_id_type=MESH,
            ).wait_recv()

    @pl.when(not_root)
    def _():
        def body(k, _):
            p_copy(sib_n, k, sib_send, sib_recv, sib).wait_recv()
            p_copy(lax.rem(sib_n + 2, 4), k, rel_send, rel_recv, sib).wait_recv()
            return 0

        lax.fori_loop(0, CH, body, 0)

    r_ref[...] = rs_ref[...]

    @pl.when(heads)
    def _():
        for i in range(7):
            t_copy(0, i, col).wait_send()
            t_copy(1, i, col).wait_send()
            rk_copy(i).wait_send()

    for i in range(7):
        c_copy(i).wait_send()
        rz_copy(i).wait_send()
    for i in range(3):
        rg_copy(i).wait_send()

    def sent(k, _):
        @pl.when(has_dn)
        def _():
            p_copy(q, k, dn_send, own_recv, dn_to).wait_send()

        @pl.when(at_zero)
        def _():
            p_copy(q, k, dn2_send, own_recv, dn2_to).wait_send()

        @pl.when(to_opp)
        def _():
            p_copy(q, k, y_send, y_recv, opp).wait_send()

        @pl.when(to_sib)
        def _():
            p_copy(q, k, sib_send, sib_recv, sib).wait_send()
            p_copy(opp_n, k, rel_send, rel_recv, sib).wait_send()

        @pl.when(is_root)
        def _():
            for n in (1, 2, 3):
                root_copy(n, k).wait_send()

        return 0

    lax.fori_loop(0, CH, sent, 0)

    @pl.when(is_root)
    def _():
        for i in range(7):
            inv_wait(i, z_peers[i])

    @pl.when(q == 0)
    def _():
        inv_wait(7, opp)

    @pl.when(jnp.logical_or(q == 0, q == 2))
    def _():
        inv_wait(8, sib)


def dot(a, b):
    return jnp.dot(a, b, precision=highest, preferred_element_type=F32)


def dot_t(a, b):
    return lax.dot_general(
        a, b, (((1,), (1,)), ((), ())), precision=highest, preferred_element_type=F32
    )


def update(
    a_ref, p_ref, t_ref, inv_ref, rows_ref, low_ref, r_ref, rk_ref, c_ref,
    o_ref, ro_ref, co_ref, xx_ref, xl_ref, xr_ref,
):
    step = pl.program_id(0)
    me = lax.axis_index("row")
    col = lax.axis_index("col")
    keep = jnp.where(me == 0, 0.0, 1.0)
    rows = a_ref.shape[0] // 4

    @pl.when(step == 0)
    def _():
        inv = inv_ref[0:128, :]
        crossing = inv_ref[128:129, :]
        for b in range(4):
            x = dot(inv, t_ref[b])
            if b == 0:
                i0 = lax.broadcasted_iota(jnp.int32, (128, 128), 0)
                i1 = lax.broadcasted_iota(jnp.int32, (128, 128), 1)
                low = jnp.where(i0 > i1, low_ref[...], jnp.where(i0 == i1, 1.0, 0.0))
                x = jnp.where(me == 0, -dot(inv, low), x)
            hi = x.astype(BF16)
            at = slice(128 * b, 128 * b + 128)
            xx_ref[0:128, at] = hi
            xx_ref[128:256, at] = hi
            xl_ref[:, at] = (x - hi.astype(F32)).astype(BF16)
            c = c_ref[b : b + 1, :]
            if b == 0:
                c = jnp.where(me == 0, 0.0, c)
            co_ref[b : b + 1, :] = c - dot(jnp.broadcast_to(crossing, (8, 128)), x)[0:1, :]
        rk = jnp.concatenate([rk_ref[0, :, 0:64], rk_ref[1, :, 0:64]], axis=1)
        xr_ref[...] = dot_t(jnp.broadcast_to(rk[0:1, :], (8, 128)), inv)

    p = p_ref[...]
    hi = p.astype(BF16)
    lo = (p - hi.astype(F32)).astype(BF16)
    both = jnp.concatenate([hi, lo], axis=1)
    d = jnp.dot(both, xx_ref[...], preferred_element_type=F32)
    d = d + jnp.dot(hi, xl_ref[...], preferred_element_type=F32)
    for b in range(4):
        a = a_ref[pl.ds(b, rows, 4), :]
        if b == 0:
            a = jnp.where(me == 0, 0.0, a)
        o_ref[pl.ds(b, rows, 4), :] = a - d[:, 128 * b : 128 * b + 128]
    e = dot_t(xr_ref[...], p)
    for t in range(rows // 64):
        at = step * (rows // 64) + t
        ro_ref[pl.ds(at, 1), :] = r_ref[pl.ds(at, 1), 0:64] - e[0:1, 64 * t : 64 * t + 64]

    @pl.when(jnp.logical_and(step == 0, col < 2))
    def _():
        at = pl.ds(pl.multiple_of(jnp.minimum(col, 1) * 64, 64), 64)
        i0 = lax.broadcasted_iota(jnp.int32, (64, 128), 0) + col * 64
        i1 = lax.broadcasted_iota(jnp.int32, (64, 128), 1)
        kept = rows_ref[at, :]
        lin = jnp.where(i0 > i1, kept, jnp.where(i0 == i1, 1.0, 0.0))
        for b in range(4):
            u = dot(lin, t_ref[b])
            if b == 0:
                u = jnp.where(me == 0, jnp.where(i0 > i1, low_ref[at, :], kept), u)
            o_ref[pl.ds(b, 64, 4), :] = u
        rk = jnp.concatenate([rk_ref[0, :, 0:64], rk_ref[1, :, 0:64]], axis=1)
        ro_ref[0:1, :] = dot_t(jnp.broadcast_to(rk[0:1, :], (8, 128)), lin)[0:1, :]


def per_device(matrix, column_weight, row_weight):
    n_rows = matrix.shape[0] * matrix.shape[2]
    dma = pltpu.SemaphoreType.DMA
    shapes = [
        (n_rows, 128), (4, 128, 128), (136, 128), (128, 128), (128, 128),
        (32, 128), (2, 8, 128), (8, 128),
    ]
    vmem = pl.BlockSpec(memory_space=pltpu.VMEM)
    got = pl.pallas_call(
        exchange,
        out_shape=[jax.ShapeDtypeStruct(s, F32) for s in shapes],
        in_specs=[pl.BlockSpec(memory_space=pltpu.HBM)] * 3,
        out_specs=[vmem] * len(shapes),
        scratch_shapes=[
            pltpu.VMEM((4, n_rows, 128), F32),
            pltpu.VMEM((4, 128), F32),
            pltpu.VMEM((32, 64), F32),
            pltpu.VMEM((3, 8, 128), F32),
            pltpu.VMEM((8, 8, 128), F32),
            pltpu.VMEM((32, 128), F32),
            pltpu.VMEM((8, 8, 128), F32),
            dma((6,)), dma((14,)), dma((4,)),
            dma((CH,)), dma((CH,)), dma((CH,)), dma((CH,)),
            dma((CH,)), dma((CH,)), dma((CH,)), dma((CH,)), dma((CH,)), dma((3 * CH,)),
            dma((3,)), dma((3,)), dma((7,)), dma((7,)), dma((3,)), dma((3,)),
            dma((7,)), dma((2,)), dma((7,)), dma((7,)), dma((9,)), dma((1,)),
            dma((9,)), dma((1,)),
        ],
        compiler_params=pltpu.CompilerParams(
            collective_id=0, has_side_effects=True, vmem_limit_bytes=24 << 20
        ),
        name="exchange",
    )(
        matrix.reshape(n_rows, 4, 128),
        column_weight.reshape(4, 128),
        row_weight.reshape(32, 64),
    )
    rows = n_rows // STEPS
    whole = lambda s: pl.BlockSpec(s, lambda i: (0,) * len(s))
    out, r, c = pl.pallas_call(
        update,
        grid=(STEPS,),
        out_shape=[
            jax.ShapeDtypeStruct((n_rows * 4, 128), F32),
            jax.ShapeDtypeStruct((32, 64), F32),
            jax.ShapeDtypeStruct((4, 128), F32),
        ],
        in_specs=[
            pl.BlockSpec((rows * 4, 128), lambda i: (i, 0)),
            pl.BlockSpec((rows, 128), lambda i: (i, 0)),
        ]
        + [whole(s) for s in shapes[1:]],
        out_specs=[
            pl.BlockSpec((rows * 4, 128), lambda i: (i, 0)),
            whole((32, 64)),
            whole((4, 128)),
        ],
        scratch_shapes=[
            pltpu.VMEM((256, 512), BF16),
            pltpu.VMEM((128, 512), BF16),
            pltpu.VMEM((8, 128), F32),
        ],
        compiler_params=pltpu.CompilerParams(vmem_limit_bytes=24 << 20),
        name="update",
    )(matrix.reshape(n_rows * 4, 128), *got)
    return (
        out.reshape(matrix.shape),
        r.reshape(row_weight.shape),
        c.reshape(column_weight.shape),
    )


def solution(mesh):
    return jax.shard_map(
        per_device,
        mesh=mesh,
        in_specs=(
            P(None, "col", None, None, "row", None),
            P(None, "row", None),
            P(None, "col", None),
        ),
        out_specs=(
            P(None, "col", None, None, "row", None),
            P(None, "col", None),
            P(None, "row", None),
        ),
        check_vma=False,
    )
```

time: 1230 us -> 59.5 us (0.05)
  the two profiles are of different devices: /device:TPU:135 before, /device:TPU:57 now
where the time goes in v1:
time: 59.5 us; the launch traced here: 59.3 us
  Pallas kernels  55.1 us (93%)
  local copies, waits for them, and re-layouts  3.58 us (6%)
  between operations  0.65 us (1%)
    pallas_call x1, Pallas kernels, per_device(): pl.pallas_call(exchange, out_shape=[jax.ShapeDtypeStruct(s, F32) for s in...  48.5 us
    pallas_call x1, Pallas kernels, per_device(): pl.pallas_call(update, grid=(STEPS,), out_shape=[jax.ShapeDtypeStruct((n_...  6.6 us
    unnamed x6, local copies, waits for them, and re-layouts  3.58 us

profile of v1, /device:TPU:57, one launch (start us, length us, event | category | flops | bytes accessed | tf_op | source)
XLA Modules:
  0.0 59.3 jit_solution(11512176143207530285)
XLA Ops:
  0.6 0.0 copy-start
  0.6 2.2 %copy-done = f32[32,1,64,4,1,128]{5,4,3,2,1,0:T(1,128)S(1)} copy-done((f32[32,1,64,4,1,128]{5,4,3,2,1,0:T(1,128)S(1)}, f32[32,1,64,4,1,128]{5,4,3,2,1,0:T(1,128)}, u32[]{:S(2)}) %copy-start) | copy-done | bytes 4194328
  2.8 0.0 copy-start.1
  2.8 0.7 %copy-done.1 = f32[32,1,64]{2,1,0:T(1,128)S(1)} copy-done((f32[32,1,64]{2,1,0:T(1,128)S(1)}, f32[32,1,64]{2,1,0:T(1,128)}, u32[]{:S(2)}) %copy-start.1) | copy-done | bytes 8216
  3.5 0.0 copy-start.2
  3.5 0.7 %copy-done.2 = f32[4,1,128]{2,1,0:T(1,128)S(1)} copy-done((f32[4,1,128]{2,1,0:T(1,128)S(1)}, f32[4,1,128]{2,1,0:T(1,128)}, u32[]{:S(2)}) %copy-start.2) | copy-done | bytes 2072
  4.2 48.5 %exchange.1 = (f32[2048,128]{1,0:T(8,128)S(1)}, f32[4,128,128]{2,1,0:T(8,128)S(1)}, f32[136,128]{1,0:T(8,128)S(1)}, f32[128,128]{1,0:T(8,128)S(1)}, f32[128,128]...) custom-call(f32[2048,4,128]{2,1,0:T(4,128)S(1)} %bitcast.13, ...), custom_call_target="tpu_custom_call" | custom-call | tf_op jit(solution)/shard_map/exchange/pallas_call | solution.py:531
  52.7 6.6 %update.1 = (f32[8192,128]{1,0:T(8,128)}, f32[32,64]{1,0:T(8,128)}, f32[4,128]{1,0:T(4,128)}) custom-call(f32[8192,128]{1,0:T(8,128)S(1)} %bitcast.14, f32[2048,128]{1,0:T(8,128)S(1)} %get-tuple-element.14.p_ref, f32[4,128,128]{2,1,0:T(8,128)S(1)} %get-tuple-element.15.t_ref, f32[136,128]{1,0:T(8,128)S(1)} %get-tuple-element.16.inv_ref, ...), custom_call_target="tpu_custom_call" | custom-call | tf_op jit(solution)/shard_map/update/pallas_call | solution.py:562
Async XLA Ops:
  0.6 2.2 %copy-start = (f32[32,1,64,4,1,128]{5,4,3,2,1,0:T(1,128)S(1)}, f32[32,1,64,4,1,128]{5,4,3,2,1,0:T(1,128)}, u32[]{:S(2)}) copy-start(f32[32,1,64,4,1,128]{5,4,3,2,1,0:T(1,128)} %param.3) | copy-start | bytes 12582916
  2.8 0.7 %copy-start.1 = (f32[32,1,64]{2,1,0:T(1,128)S(1)}, f32[32,1,64]{2,1,0:T(1,128)}, u32[]{:S(2)}) copy-start(f32[32,1,64]{2,1,0:T(1,128)} %param.5) | copy-start | bytes 24580
  3.5 0.7 %copy-start.2 = (f32[4,1,128]{2,1,0:T(1,128)S(1)}, f32[4,1,128]{2,1,0:T(1,128)}, u32[]{:S(2)}) copy-start(f32[4,1,128]{2,1,0:T(1,128)} %param.4) | copy-start | bytes 6148

commit v2 on v1

--- a/solution.py
+++ b/solution.py
@@ -14,51 +14,77 @@
 STEPS = 8
 
 
-def spread_lane(x, i):
-    return jnp.broadcast_to(x[:, i : i + 1], (8, 128))
-
-
-def eliminate(g_ref, inv_ref, rows_ref, low_ref):
+def dot(a, b):
+    return jnp.dot(a, b, precision=highest, preferred_element_type=F32)
+
+
+def dot_t(a, b):
+    return lax.dot_general(
+        a, b, (((1,), (1,)), ((), ())), precision=highest, preferred_element_type=F32
+    )
+
+
+def eliminate(g_ref, inv_ref, rows_ref, cols_ref, diag_ref):
     lane = lax.broadcasted_iota(jnp.int32, (8, 128), 1)
     sub = lax.broadcasted_iota(jnp.int32, (8, 128), 0)
-    low_ref[...] = jnp.zeros((128, 128), F32)
-
-    def strip(s, vs):
-        vs = list(vs)
-        cols = [jnp.zeros((8, 128), F32)] * 16
-        kept = jnp.zeros((8, 128), F32)
+    full = (8, 128)
+    vs = [g_ref[8 * j : 8 * j + 8, :] for j in range(16)]
+    kept_cols = [jnp.zeros(full, F32) for _ in range(16)]
+    for s in range(16):
+        base = 8 * s
+        inside = jnp.logical_and(lane >= base, lane < base + 8)
+        v0 = vs[s]
+        cs = [jnp.broadcast_to(v0[:, base + j : base + j + 1], full) for j in range(8)]
+        factors = [
+            [jnp.broadcast_to(vs[r][:, base + j : base + j + 1], full) for j in range(8)]
+            if r != s else None
+            for r in range(16)
+        ]
+        v = v0
+        diag = jnp.zeros(full, F32)
         for i in range(8):
-            row = jnp.broadcast_to(vs[0][i : i + 1, :], (8, 128))
-            here = lane == i
-            recip = 1.0 / spread_lane(row, i)
-            scaled = jnp.where(here, recip, row * recip)
-            kept = jnp.where(sub == i, row, kept)
-            for j in range(16):
-                new = jnp.where(here, 0.0, vs[j]) - spread_lane(vs[j], i) * scaled
-                cols[j] = jnp.where(here, -new, cols[j])
-                if j == 0:
-                    new = jnp.where(sub == i, scaled, new)
-                vs[j] = new
-        turn = s * 8
-        rows_ref[pl.ds(pl.multiple_of(turn, 8), 8), :] = pltpu.roll(kept, turn, 1)
-        for j in range(16):
-            at = pl.multiple_of(lax.rem(s + j, 16) * 8, 8)
-            low_ref[pl.ds(at, 8), :] += pltpu.roll(
-                jnp.where(lane < 8, cols[j], 0.0), turn, 1
-            )
-        return tuple(pltpu.roll(x, 120, 1) for x in vs[1:] + vs[:1])
-
-    out = lax.fori_loop(
-        0, 16, strip, tuple(g_ref[8 * j : 8 * j + 8, :] for j in range(16))
-    )
+            here = lane == base + i
+            at_i = sub == i
+            under = sub > i
+            recip = 1.0 / jnp.broadcast_to(cs[i][i : i + 1, :], full)
+            ratio = cs[i] * recip
+            down = jnp.where(under, ratio, 0.0)
+            row = jnp.broadcast_to(v[i : i + 1, :], full)
+            v = jnp.where(jnp.logical_and(here, under), -ratio, v - down * jnp.where(here, 0.0, row))
+            diag = jnp.where(here, down, diag)
+            for j in range(8):
+                if j != i:
+                    t = jnp.broadcast_to(cs[j][i : i + 1, :], full)
+                    cs[j] = jnp.where(at_i, t * recip, cs[j] - ratio * t)
+            cs[i] = jnp.where(at_i, recip, -ratio)
+        rows_ref[base : base + 8, :] = v
+        diag_ref[base : base + 8, :] = diag
+        v0 = jnp.where(inside, jnp.where(lane - base == sub, 1.0, 0.0), v0)
+        w = cs[0] * jnp.broadcast_to(v0[0:1, :], full)
+        for j in range(1, 8):
+            w = w + cs[j] * jnp.broadcast_to(v0[j : j + 1, :], full)
+        wr = [jnp.broadcast_to(w[j : j + 1, :], full) for j in range(8)]
+        order = [r % 16 for r in range(s + 1, s + 16)]
+        for r in order:
+            f = factors[r]
+            a = f[0] * wr[0] + f[1] * wr[1]
+            b = f[2] * wr[2] + f[3] * wr[3]
+            c = f[4] * wr[4] + f[5] * wr[5]
+            d = f[6] * wr[6] + f[7] * wr[7]
+            new = jnp.where(inside, 0.0, vs[r]) - ((a + b) + (c + d))
+            vs[r] = new
+            if r > s:
+                kept_cols[r] = jnp.where(inside, new, kept_cols[r])
+        vs[s] = w
     for j in range(16):
-        inv_ref[8 * j : 8 * j + 8, :] = out[j]
+        inv_ref[8 * j : 8 * j + 8, :] = vs[j]
+        cols_ref[8 * j : 8 * j + 8, :] = kept_cols[j]
 
 
 def exchange(
     a_hbm, w_hbm, v_hbm,
-    p_ref, t_ref, inv_ref, rows_ref, low_ref, r_ref, rk_ref, c_ref,
-    a_ref, w_ref, v_ref, rq_ref, rz_ref, rs_ref, cz_ref,
+    p_ref, t_ref, inv_ref, rows_ref, low_ref, uin_ref, r_ref, rk_ref, c_ref,
+    cols_ref, diag_ref, a_ref, w_ref, v_ref, rq_ref, rz_ref, rs_ref, cz_ref,
     load_sem, t_send, t_recv, own_recv, sib_recv, y_recv, rel_recv,
     dn_send, dn2_send, sib_send, y_send, rel_send, root_send,
     rq_send, rq_recv, rz_send, rz_recv, rg_send, rg_recv, rk_send, rk_recv,
@@ -107,7 +133,9 @@
         return tuple(out)
 
     r_ref[...] = jnp.zeros((32, 128), F32)
-    acc = lax.fori_loop(0, 32, sums, tuple(jnp.zeros((8, 128), F32) for _ in range(4)))
+    acc = lax.fori_loop(
+        0, 32, sums, tuple(jnp.zeros((8, 128), F32) for _ in range(4)), unroll=4
+    )
     for b in range(4):
         c_ref[b : b + 1, :] = jnp.sum(acc[b], axis=0, keepdims=True)
     c_ref[4:8, :] = jnp.zeros((4, 128), F32)
@@ -268,7 +296,7 @@
             @pl.when(col != s)
             def _():
                 t_copy(0, 0, s).wait_recv()
-        eliminate(t_ref.at[0], inv_ref.at[pl.ds(0, 128)], rows_ref, low_ref)
+        eliminate(t_ref.at[0], inv_ref, rows_ref, cols_ref, diag_ref)
 
     def rg_copy(i):
         return pltpu.make_async_remote_copy(
@@ -321,6 +349,15 @@
             inv_to(i, z_peers[i])
         inv_to(7, opp)
         inv_to(8, sib)
+
+    @pl.when(is_root)
+    def _():
+        i0 = lax.broadcasted_iota(jnp.int32, (128, 128), 0)
+        i1 = lax.broadcasted_iota(jnp.int32, (128, 128), 1)
+        inner = diag_ref[...] + jnp.where(i0 == i1, 1.0, 0.0)
+        low = jnp.where(i0 // 8 > i1 // 8, -dot(cols_ref[...], inner), inner)
+        low_ref[...] = low
+        uin_ref[...] = -dot(inv_ref[0:128, :], low)
 
     for i in range(7):
         rz_arrival(i).wait_recv()
@@ -445,18 +482,8 @@
         inv_wait(8, sib)
 
 
-def dot(a, b):
-    return jnp.dot(a, b, precision=highest, preferred_element_type=F32)
-
-
-def dot_t(a, b):
-    return lax.dot_general(
-        a, b, (((1,), (1,)), ((), ())), precision=highest, preferred_element_type=F32
-    )
-
-
 def update(
-    a_ref, p_ref, t_ref, inv_ref, rows_ref, low_ref, r_ref, rk_ref, c_ref,
+    a_ref, p_ref, t_ref, inv_ref, rows_ref, low_ref, uin_ref, r_ref, rk_ref, c_ref,
     o_ref, ro_ref, co_ref, xx_ref, xl_ref, xr_ref,
 ):
     step = pl.program_id(0)
@@ -472,10 +499,7 @@
         for b in range(4):
             x = dot(inv, t_ref[b])
             if b == 0:
-                i0 = lax.broadcasted_iota(jnp.int32, (128, 128), 0)
-                i1 = lax.broadcasted_iota(jnp.int32, (128, 128), 1)
-                low = jnp.where(i0 > i1, low_ref[...], jnp.where(i0 == i1, 1.0, 0.0))
-                x = jnp.where(me == 0, -dot(inv, low), x)
+                x = jnp.where(me == 0, uin_ref[...], x)
             hi = x.astype(BF16)
             at = slice(128 * b, 128 * b + 128)
             xx_ref[0:128, at] = hi
@@ -520,11 +544,15 @@
         ro_ref[0:1, :] = dot_t(jnp.broadcast_to(rk[0:1, :], (8, 128)), lin)[0:1, :]
 
 
+def in_hbm(x):
+    return pltpu.with_memory_space_constraint(x, pltpu.HBM)
+
+
 def per_device(matrix, column_weight, row_weight):
     n_rows = matrix.shape[0] * matrix.shape[2]
     dma = pltpu.SemaphoreType.DMA
     shapes = [
-        (n_rows, 128), (4, 128, 128), (136, 128), (128, 128), (128, 128),
+        (n_rows, 128), (4, 128, 128), (136, 128), (128, 128), (128, 128), (128, 128),
         (32, 128), (2, 8, 128), (8, 128),
     ]
     vmem = pl.BlockSpec(memory_space=pltpu.VMEM)
@@ -534,6 +562,8 @@
         in_specs=[pl.BlockSpec(memory_space=pltpu.HBM)] * 3,
         out_specs=[vmem] * len(shapes),
         scratch_shapes=[
+            pltpu.VMEM((128, 128), F32),
+            pltpu.VMEM((128, 128), F32),
             pltpu.VMEM((4, n_rows, 128), F32),
             pltpu.VMEM((4, 128), F32),
             pltpu.VMEM((32, 64), F32),
@@ -553,9 +583,9 @@
         ),
         name="exchange",
     )(
-        matrix.reshape(n_rows, 4, 128),
-        column_weight.reshape(4, 128),
-        row_weight.reshape(32, 64),
+        in_hbm(matrix.reshape(n_rows, 4, 128)),
+        in_hbm(column_weight.reshape(4, 128)),
+        in_hbm(row_weight.reshape(32, 64)),
     )
     rows = n_rows // STEPS
     whole = lambda s: pl.BlockSpec(s, lambda i: (0,) * len(s))

time: 59.5 us -> 49.6 us (0.83)
  the two profiles are of different devices: /device:TPU:57 before, /device:TPU:155 now
where the time goes in v2:
time: 49.6 us; the launch traced here: 49.5 us
  Pallas kernels  48.9 us (99%)
  between operations  0.65 us (1%)
    pallas_call x1, Pallas kernels, per_device(): pl.pallas_call(exchange, out_shape=[jax.ShapeDtypeStruct(s, F32) for s in...  42.7 us
    pallas_call x1, Pallas kernels, per_device(): pl.pallas_call(update, grid=(STEPS,), out_shape=[jax.ShapeDtypeStruct((n_...  6.22 us

profile of v2, /device:TPU:155, one launch (start us, length us, event | category | flops | bytes accessed | tf_op | source)
XLA Modules:
  0.0 49.5 jit_solution(5958034379365225515)
XLA Ops:
  0.6 0.0 copy-start
  0.6 42.7 %exchange.1 = (f32[2048,128]{1,0:T(8,128)S(1)}, f32[4,128,128]{2,1,0:T(8,128)S(1)}, f32[136,128]{1,0:T(8,128)S(1)}, f32[128,128]{1,0:T(8,128)S(1)}, f32[128,128]...) custom-call(f32[2048,4,128]{2,1,0:T(4,128)} %bitcast.13, ...), custom_call_target="tpu_custom_call" | custom-call | tf_op jit(solution)/shard_map/exchange/pallas_call | solution.py:559
  43.3 0.0 copy-done
  43.3 6.2 %update.1 = (f32[8192,128]{1,0:T(8,128)}, f32[32,64]{1,0:T(8,128)}, f32[4,128]{1,0:T(4,128)}) custom-call(f32[8192,128]{1,0:T(8,128)S(1)} %bitcast.14, f32[2048,128]{1,0:T(8,128)S(1)} %get-tuple-element.15.p_ref, f32[4,128,128]{2,1,0:T(8,128)S(1)} %get-tuple-element.16.t_ref, f32[136,128]{1,0:T(8,128)S(1)} %get-tuple-element.17.inv_ref, ...), custom_call_target="tpu_custom_call" | custom-call | tf_op jit(solution)/shard_map/update/pallas_call | solution.py:592
Async XLA Ops:
  0.6 42.7 %copy-start = (f32[32,1,64,4,1,128]{5,4,3,2,1,0:T(1,128)S(1)}, f32[32,1,64,4,1,128]{5,4,3,2,1,0:T(1,128)}, u32[]{:S(2)}) copy-start(f32[32,1,64,4,1,128]{5,4,3,2,1,0:T(1,128)} %param.3) | copy-start | bytes 12582916

commit v3 on v2

v3 whole, which is shorter than its diff:
```python
import jax
import jax.numpy as jnp
from jax import lax
from jax.experimental import pallas as pl
from jax.experimental.pallas import tpu as pltpu
from jax.sharding import PartitionSpec as P

MESH = pl.DeviceIdType.MESH
highest = lax.Precision.HIGHEST
F32 = jnp.float32
BF16 = jnp.bfloat16
NZ = 8
CH = 8
STEPS = 8


def dot(a, b):
    return jnp.dot(a, b, precision=highest, preferred_element_type=F32)


def dot_t(a, b):
    return lax.dot_general(
        a, b, (((1,), (1,)), ((), ())), precision=highest, preferred_element_type=F32
    )


def eliminate(g_ref, inv_ref, rows_ref, cols_ref, diag_ref):
    lane = lax.broadcasted_iota(jnp.int32, (8, 128), 1)
    sub = lax.broadcasted_iota(jnp.int32, (8, 128), 0)
    full = (8, 128)
    vs = [g_ref[8 * j : 8 * j + 8, :] for j in range(16)]
    kept_cols = [jnp.zeros(full, F32) for _ in range(16)]
    for s in range(16):
        base = 8 * s
        inside = jnp.logical_and(lane >= base, lane < base + 8)
        v0 = vs[s]
        cs = [jnp.broadcast_to(v0[:, base + j : base + j + 1], full) for j in range(8)]
        factors = [
            [jnp.broadcast_to(vs[r][:, base + j : base + j + 1], full) for j in range(8)]
            if r != s else None
            for r in range(16)
        ]
        v = v0
        diag = jnp.zeros(full, F32)
        for i in range(8):
            here = lane == base + i
            at_i = sub == i
            under = sub > i
            recip = 1.0 / jnp.broadcast_to(cs[i][i : i + 1, :], full)
            ratio = cs[i] * recip
            down = jnp.where(under, ratio, 0.0)
            row = jnp.broadcast_to(v[i : i + 1, :], full)
            v = jnp.where(jnp.logical_and(here, under), -ratio, v - down * jnp.where(here, 0.0, row))
            diag = jnp.where(here, down, diag)
            for j in range(8):
                if j != i:
                    t = jnp.broadcast_to(cs[j][i : i + 1, :], full)
                    cs[j] = jnp.where(at_i, t * recip, cs[j] - ratio * t)
            cs[i] = jnp.where(at_i, recip, -ratio)
        rows_ref[base : base + 8, :] = v
        diag_ref[base : base + 8, :] = diag
        v0 = jnp.where(inside, jnp.where(lane - base == sub, 1.0, 0.0), v0)
        w = cs[0] * jnp.broadcast_to(v0[0:1, :], full)
        for j in range(1, 8):
            w = w + cs[j] * jnp.broadcast_to(v0[j : j + 1, :], full)
        wr = [jnp.broadcast_to(w[j : j + 1, :], full) for j in range(8)]
        order = [r % 16 for r in range(s + 1, s + 16)]
        for r in order:
            f = factors[r]
            a = f[0] * wr[0] + f[1] * wr[1]
            b = f[2] * wr[2] + f[3] * wr[3]
            c = f[4] * wr[4] + f[5] * wr[5]
            d = f[6] * wr[6] + f[7] * wr[7]
            new = jnp.where(inside, 0.0, vs[r]) - ((a + b) + (c + d))
            vs[r] = new
            if r > s:
                kept_cols[r] = jnp.where(inside, new, kept_cols[r])
        vs[s] = w
    for j in range(16):
        inv_ref[8 * j : 8 * j + 8, :] = vs[j]
        cols_ref[8 * j : 8 * j + 8, :] = kept_cols[j]


def exchange(
    a_hbm, w_hbm, v_hbm,
    p_ref, xx_ref, xl_ref, xr_ref, u_ref, r_ref, c_ref,
    t_ref, inv_ref, rows_ref, low_ref, rk_ref,
    cols_ref, diag_ref, a_ref, w_ref, v_ref, rq_ref, rz_ref, rs_ref, cz_ref,
    load_sem, t_send, t_recv, own_recv, sib_recv, y_recv, rel_recv,
    dn_send, dn2_send, sib_send, y_send, rel_send, root_send,
    rq_send, rq_recv, rz_send, rz_recv, rg_send, rg_recv, rk_send, rk_recv,
    c_send, c_recv, i_send, i_recv, l_send, l_recv,
    dn_ready, dn2_ready, z_ready, z_go,
):
    me = lax.axis_index("row")
    col = lax.axis_index("col")
    z = me // 4
    q = lax.rem(me, 4)
    is_root = me == 0
    not_root = jnp.logical_not(is_root)
    heads = col < 2
    at_zero = z == 0
    off_zero = z > 0

    def at_row(r):
        return dict(row=r, col=col)

    z_peers = [at_row(lax.rem(z + d, NZ) * 4 + q) for d in range(1, NZ)]
    q_peers = [at_row(z * 4 + lax.rem(q + d, 4)) for d in range(1, 4)]
    c_peers = [dict(row=me, col=lax.rem(col + d, 8)) for d in range(1, 8)]
    sib_n = q + 1 - 2 * lax.rem(q, 2)
    opp_n = lax.rem(q + 2, 4)
    sib = at_row(z * 4 + sib_n)
    opp = at_row(z * 4 + opp_n)
    has_dn = jnp.logical_and(z != 4, z != 5)
    dn_to = at_row(jnp.where(z < 4, z + 1, jnp.where(has_dn, z - 1, z + 1)) * 4 + q)
    dn2_to = at_row(7 * 4 + q)
    up_from = at_row(jnp.where(z > 4, lax.rem(z + 1, NZ), jnp.where(off_zero, z - 1, z + 1)) * 4 + q)

    def signal(sem, to):
        pl.semaphore_signal(sem, inc=1, device_id=to, device_id_type=MESH)

    loads = [
        pltpu.make_async_copy(a_hbm.at[:, b, :], a_ref.at[b], load_sem.at[b])
        for b in range(4)
    ]
    loads.append(pltpu.make_async_copy(w_hbm, w_ref, load_sem.at[4]))
    loads.append(pltpu.make_async_copy(v_hbm, v_ref, load_sem.at[5]))
    for x in loads:
        x.start()

    barrier = pltpu.get_barrier_semaphore()
    for x in q_peers + c_peers:
        signal(barrier, x)

    @pl.when(at_zero)
    def _():
        for x in z_peers:
            signal(barrier, x)

    @pl.when(jnp.logical_and(off_zero, has_dn))
    def _():
        signal(barrier, dn_to)

    for x in loads:
        x.wait()

    def sums(t, acc):
        at = pl.multiple_of(t * 64, 64)
        v = jnp.broadcast_to(v_ref[pl.ds(t, 1), :], (128, 64)).T
        across = jnp.zeros((64, 128), F32)
        out = []
        for b in range(4):
            block = a_ref[b, pl.ds(at, 64), :]
            across = across + block * w_ref[b : b + 1, :]
            out.append(acc[b] + (block * v).reshape(8, 8, 128).sum(0))
        r_ref[pl.ds(t, 1), 0:64] = jnp.sum(across.T, axis=0, keepdims=True)
        return tuple(out)

    r_ref[...] = jnp.zeros((32, 128), F32)
    acc = lax.fori_loop(
        0, 32, sums, tuple(jnp.zeros((8, 128), F32) for _ in range(4)), unroll=4
    )
    for b in range(4):
        c_ref[b : b + 1, :] = jnp.sum(acc[b], axis=0, keepdims=True)
    c_ref[4:8, :] = jnp.zeros((4, 128), F32)

    @pl.when(is_root)
    def _():
        p_ref[...] = a_ref[0]

    pl.semaphore_wait(
        barrier, 10 + jnp.where(at_zero, 0, 1) + jnp.where(jnp.logical_and(z > 1, z < 7), 1, 0)
    )

    @pl.when(off_zero)
    def _():
        @pl.when(z == 7)
        def _():
            signal(dn2_ready, up_from)

        @pl.when(z != 7)
        def _():
            signal(dn_ready, up_from)

        signal(z_ready, at_row(q))

    @pl.when(heads)
    def _():
        mine = pl.ds(pl.multiple_of(col * 64, 64), 64)
        t_ref[:, mine, :] = a_ref[:, 0:64, :]

    def t_copy(part, i, src):
        blocks = pl.ds(0, 1) if part == 0 else pl.ds(1, 3)
        mine = pl.ds(pl.multiple_of(src * 64, 64), 64)
        return pltpu.make_async_remote_copy(
            t_ref.at[blocks, mine, :], t_ref.at[blocks, mine, :],
            t_send.at[part * 7 + i], t_recv.at[part * 2 + src],
            device_id=c_peers[i], device_id_type=MESH,
        )

    @pl.when(heads)
    def _():
        for i in range(7):
            t_copy(0, i, col).start()

    def piece(n, k):
        return pl.ds(pl.multiple_of(n * (CH * 64) + k * 64, 64), 64)

    def p_copy(n, k, send, recv, to):
        return pltpu.make_async_remote_copy(
            p_ref.at[piece(n, k)], p_ref.at[piece(n, k)],
            send.at[k], recv.at[k], device_id=to, device_id_type=MESH,
        )

    to_sib = jnp.logical_not(jnp.logical_and(at_zero, q == 1))
    to_opp = jnp.logical_not(jnp.logical_and(at_zero, q == 2))

    def pass_dn2(k, _):
        p_copy(q, k, dn2_send, own_recv, dn2_to).start()
        return 0

    def pass_quad(k):
        @pl.when(to_opp)
        def _():
            p_copy(q, k, y_send, y_recv, opp).start()

        @pl.when(to_sib)
        def _():
            p_copy(q, k, sib_send, sib_recv, sib).start()

    def pass_opp(k):
        @pl.when(to_sib)
        def _():
            p_copy(opp_n, k, rel_send, rel_recv, sib).start()

    def root_copy(n, k):
        return pltpu.make_async_remote_copy(
            p_ref.at[piece(n, k)], p_ref.at[piece(n, k)],
            root_send.at[(n - 1) * CH + k], own_recv.at[k],
            device_id=at_row(n), device_id_type=MESH,
        )

    @pl.when(is_root)
    def _():
        def out(k, _):
            for n in (2, 3, 1):
                root_copy(n, k).start()
            return 0

        lax.fori_loop(0, CH, out, 0)

    cz_ref[pl.ds(col, 1)] = c_ref[...][None]

    def c_copy(i):
        return pltpu.make_async_remote_copy(
            cz_ref.at[col], cz_ref.at[col], c_send.at[i], c_recv.at[i],
            device_id=c_peers[i], device_id_type=MESH,
        )

    for i in range(7):
        c_copy(i).start()

    def rq_copy(i):
        to = lax.rem(q + i + 1, 4)
        return pltpu.make_async_remote_copy(
            r_ref.at[pl.ds(pl.multiple_of(to * 8, 8), 8)], rq_ref.at[i],
            rq_send.at[i], rq_recv.at[i],
            device_id=q_peers[i], device_id_type=MESH,
        )

    for i in range(3):
        rq_copy(i).start()

    @pl.when(at_zero)
    def _():
        pl.semaphore_wait(dn_ready, 1)

    @pl.when(is_root)
    def _():
        def out(k, _):
            p_copy(q, k, dn_send, own_recv, dn_to).start()
            pass_quad(k)
            pass_opp(k)
            return 0

        lax.fori_loop(0, CH, out, 0)

    @pl.when(heads)
    def _():
        for i in range(7):
            t_copy(1, i, col).start()

    quarter = pl.ds(pl.multiple_of(q * 8, 8), 8)

    def rz_copy(i):
        return pltpu.make_async_remote_copy(
            rz_ref.at[z], rz_ref.at[z], rz_send.at[i], rz_recv.at[i],
            device_id=z_peers[i], device_id_type=MESH,
        )

    def rz_arrival(i):
        return pltpu.make_async_remote_copy(
            rz_ref.at[z], rz_ref.at[lax.rem(z + NZ - 1 - i, NZ)], rz_send.at[i], rz_recv.at[i],
            device_id=z_peers[i], device_id_type=MESH,
        )

    def spread_quarter():
        for i in range(3):
            rq_copy(i).wait()
        total = r_ref[quarter, :] + rq_ref[0] + rq_ref[1] + rq_ref[2]
        rz_ref[pl.ds(z, 1)] = total[None]
        for i in range(7):
            rz_copy(i).start()

    def rg_copy(i):
        return pltpu.make_async_remote_copy(
            rs_ref.at[quarter], rs_ref.at[quarter], rg_send.at[i], rg_recv.at[i],
            device_id=q_peers[i], device_id_type=MESH,
        )

    def rg_arrival(i):
        theirs = pl.ds(pl.multiple_of(lax.rem(q + 3 - i, 4) * 8, 8), 8)
        return pltpu.make_async_remote_copy(
            rs_ref.at[theirs], rs_ref.at[theirs], rg_send.at[i], rg_recv.at[i],
            device_id=q_peers[i], device_id_type=MESH,
        )

    def gather_quarters():
        for i in range(7):
            rz_arrival(i).wait_recv()
        whole = rz_ref[0]
        for i in range(1, 8):
            whole = whole + rz_ref[i]
        rs_ref[quarter, :] = whole
        for i in range(3):
            rg_copy(i).start()

    def rk_copy(i):
        return pltpu.make_async_remote_copy(
            rs_ref.at[pl.ds(0, 8)], rk_ref.at[col], rk_send.at[i], rk_recv.at[col],
            device_id=c_peers[i], device_id_type=MESH,
        )

    def spread_pivot_checks():
        for i in range(3):
            rg_arrival(i).wait_recv()

        @pl.when(heads)
        def _():
            rk_ref[pl.ds(col, 1)] = rs_ref[0:8, :][None]
            for i in range(7):
                rk_copy(i).start()

    def take_own(k, _):
        p_copy(q, k, dn_send, own_recv, dn_to).wait_recv()

        @pl.when(has_dn)
        def _():
            p_copy(q, k, dn_send, own_recv, dn_to).start()

        pass_quad(k)
        return 0

    def take_opp(k, _):
        p_copy(opp_n, k, y_send, y_recv, opp).wait_recv()
        pass_opp(k)
        return 0

    def own(a, b):
        lax.fori_loop(a, b, take_own, 0)

    mine = pl.ds(pl.multiple_of(jnp.minimum(col, 1) * 64, 64), 64)

    def i_copy(i, to):
        return pltpu.make_async_remote_copy(
            inv_ref, inv_ref, i_send.at[i], i_recv.at[0], device_id=to, device_id_type=MESH
        )

    def l_copy(i, to):
        return pltpu.make_async_remote_copy(
            rows_ref.at[mine], rows_ref.at[mine], l_send.at[i], l_recv.at[0],
            device_id=to, device_id_type=MESH,
        )

    def inv_to(i, to):
        i_copy(i, to).start()

        @pl.when(heads)
        def _():
            l_copy(i, to).start()

    def inv_wait(i, to):
        i_copy(i, to).wait_send()

        @pl.when(heads)
        def _():
            l_copy(i, to).wait_send()

    even = lax.rem(q, 2) == 0
    over_z = jnp.logical_and(at_zero, even)
    z_order = (3, 4, 2, 5, 1, 0, 6)

    def take_inverse():
        i_copy(0, sib).wait_recv()

        @pl.when(heads)
        def _():
            l_copy(0, sib).wait_recv()

        @pl.when(over_z)
        def _():
            for i in z_order:
                inv_to(i, z_peers[i])

        @pl.when(even)
        def _():
            inv_to(8, sib)

    def sum_columns():
        for i in range(7):
            c_copy(i).wait_recv()
        over = cz_ref[0]
        for i in range(1, 8):
            over = over + cz_ref[i]
        c_ref[...] = over
        return over

    @pl.when(jnp.logical_and(at_zero, not_root))
    def _():
        own(0, 4)

    @pl.when(at_zero)
    def _():
        pl.semaphore_wait(dn2_ready, 1)
        pl.semaphore_wait(z_ready, 7)
        for x in z_peers:
            signal(z_go, x)

    @pl.when(is_root)
    def _():
        lax.fori_loop(0, CH, pass_dn2, 0)
        spread_quarter()
        for s in range(2):
            @pl.when(col != s)
            def _():
                t_copy(0, 0, s).wait_recv()
        eliminate(t_ref.at[0], inv_ref, rows_ref, cols_ref, diag_ref)
        inv_ref[128:136, :] = sum_columns()
        inv_to(7, opp)
        for i in z_order:
            inv_to(i, z_peers[i])
        inv_to(8, sib)
        gather_quarters()
        i0 = lax.broadcasted_iota(jnp.int32, (128, 128), 0)
        i1 = lax.broadcasted_iota(jnp.int32, (128, 128), 1)
        inner = diag_ref[...] + jnp.where(i0 == i1, 1.0, 0.0)
        low_ref[...] = jnp.where(i0 // 8 > i1 // 8, -dot(cols_ref[...], inner), inner)
        spread_pivot_checks()

    @pl.when(jnp.logical_and(at_zero, not_root))
    def _():
        lax.fori_loop(0, 4, pass_dn2, 0)
        spread_quarter()

        def both(k, _):
            take_own(k, 0)
            return pass_dn2(k, 0)

        lax.fori_loop(4, CH, both, 0)
        lax.fori_loop(0, CH, take_opp, 0)
        gather_quarters()
        take_inverse()
        spread_pivot_checks()

    near = jnp.logical_or(z == 1, z == 7)

    @pl.when(off_zero)
    def _():
        pl.semaphore_wait(z_go, 1)
        @pl.when(jnp.logical_and(has_dn, z != 0))
        def _():
            pl.semaphore_wait(dn_ready, 1)

        spread_quarter()

        @pl.when(near)
        def _():
            own(0, CH)
            gather_quarters()
            lax.fori_loop(0, CH, take_opp, 0)
            spread_pivot_checks()
            take_inverse()

        @pl.when(jnp.logical_not(near))
        def _():
            gather_quarters()
            own(0, 4)
            spread_pivot_checks()
            own(4, CH)
            take_inverse()
            lax.fori_loop(0, CH, take_opp, 0)

    @pl.when(not_root)
    def _():
        sum_columns()

    for s in range(2):
        @pl.when(col != s)
        def _():
            @pl.when(not_root)
            def _():
                t_copy(0, 0, s).wait_recv()

            t_copy(1, 0, s).wait_recv()
            pltpu.make_async_remote_copy(
                rs_ref.at[pl.ds(0, 8)], rk_ref.at[s], rk_send.at[0], rk_recv.at[s],
                device_id=c_peers[0], device_id_type=MESH,
            ).wait_recv()

    inv = inv_ref[0:128, :]
    crossing = inv_ref[128:136, :]
    for b in range(4):
        at = slice(128 * b, 128 * b + 128)
        c = c_ref[b : b + 1, :]
        if b == 0:
            @pl.when(is_root)
            def _():
                cols_ref[...] = -dot(inv, low_ref[...])

            @pl.when(not_root)
            def _():
                cols_ref[...] = dot(inv, t_ref[0])

            x = cols_ref[...]
            c = jnp.where(is_root, 0.0, c)
        else:
            x = dot(inv, t_ref[b])
        hi = x.astype(BF16)
        xx_ref[0:128, at] = hi
        xx_ref[128:256, at] = hi
        xl_ref[:, at] = (x - hi.astype(F32)).astype(BF16)
        c_ref[b : b + 1, :] = c - dot(crossing, x)[0:1, :]
    rk = jnp.concatenate([rk_ref[0, :, 0:64], rk_ref[1, :, 0:64]], axis=1)
    rk = jnp.broadcast_to(rk[0:1, :], (8, 128))
    xr_ref[:, 0:128] = dot_t(rk, inv)
    r_ref[...] = rs_ref[...]

    @pl.when(heads)
    def _():
        i0 = lax.broadcasted_iota(jnp.int32, (64, 128), 0) + col * 64
        i1 = lax.broadcasted_iota(jnp.int32, (64, 128), 1)
        kept = rows_ref[mine, :]
        lin = jnp.where(i0 > i1, kept, jnp.where(i0 == i1, 1.0, 0.0))
        for b in range(4):
            u_ref[b] = dot(lin, t_ref[b])

        @pl.when(is_root)
        def _():
            u_ref[0] = jnp.where(i0 > i1, low_ref[mine, :], kept)

        xr_ref[:, 128:192] = dot_t(rk, lin)

    @pl.when(not_root)
    def _():
        def body(k, _):
            p_copy(sib_n, k, sib_send, sib_recv, sib).wait_recv()
            p_copy(lax.rem(sib_n + 2, 4), k, rel_send, rel_recv, sib).wait_recv()
            return 0

        lax.fori_loop(0, CH, body, 0)

    @pl.when(heads)
    def _():
        for i in range(7):
            t_copy(0, i, col).wait_send()
            t_copy(1, i, col).wait_send()
            rk_copy(i).wait_send()

    for i in range(7):
        c_copy(i).wait_send()
        rz_copy(i).wait_send()
    for i in range(3):
        rg_copy(i).wait_send()

    def sent(k, _):
        @pl.when(has_dn)
        def _():
            p_copy(q, k, dn_send, own_recv, dn_to).wait_send()

        @pl.when(at_zero)
        def _():
            p_copy(q, k, dn2_send, own_recv, dn2_to).wait_send()

        @pl.when(to_opp)
        def _():
            p_copy(q, k, y_send, y_recv, opp).wait_send()

        @pl.when(to_sib)
        def _():
            p_copy(q, k, sib_send, sib_recv, sib).wait_send()
            p_copy(opp_n, k, rel_send, rel_recv, sib).wait_send()

        @pl.when(is_root)
        def _():
            for n in (1, 2, 3):
                root_copy(n, k).wait_send()

        return 0

    lax.fori_loop(0, CH, sent, 0)

    @pl.when(over_z)
    def _():
        for i in range(7):
            inv_wait(i, z_peers[i])

    @pl.when(is_root)
    def _():
        inv_wait(7, opp)

    @pl.when(even)
    def _():
        inv_wait(8, sib)


def update(
    a_ref, p_ref, xx_ref, xl_ref, xr_ref, u_ref, r_ref, c_ref, o_ref, ro_ref, co_ref
):
    step = pl.program_id(0)
    me = lax.axis_index("row")
    col = lax.axis_index("col")
    rows = a_ref.shape[0] // 4
    p = p_ref[...]
    hi = p.astype(BF16)
    lo = (p - hi.astype(F32)).astype(BF16)
    both = jnp.concatenate([hi, lo], axis=1)
    d = jnp.dot(both, xx_ref[...], preferred_element_type=F32)
    d = d + jnp.dot(hi, xl_ref[...], preferred_element_type=F32)
    for b in range(4):
        a = a_ref[pl.ds(b, rows, 4), :]
        if b == 0:
            a = jnp.where(me == 0, 0.0, a)
        o_ref[pl.ds(b, rows, 4), :] = a - d[:, 128 * b : 128 * b + 128]
    x = xr_ref[:, 0:128]
    xh = x.astype(BF16)
    xw = (x - xh.astype(F32)).astype(BF16)
    nt = (((1,), (1,)), ((), ()))
    pair = jnp.concatenate([xh, xw], axis=0)
    e = lax.dot_general(pair, hi, nt, preferred_element_type=F32)
    e = e[0:1, :] + e[8:9, :] + lax.dot_general(xh, lo, nt, preferred_element_type=F32)[0:1, :]
    for t in range(rows // 64):
        at = step * (rows // 64) + t
        ro_ref[pl.ds(at, 1), :] = r_ref[pl.ds(at, 1), 0:64] - e[:, 64 * t : 64 * t + 64]

    @pl.when(step == 0)
    def _():
        co_ref[...] = c_ref[0:4, :]

        @pl.when(col < 2)
        def _():
            for b in range(4):
                o_ref[pl.ds(b, 64, 4), :] = u_ref[b]
            ro_ref[0:1, :] = xr_ref[0:1, 128:192]


def in_hbm(x):
    return pltpu.with_memory_space_constraint(x, pltpu.HBM)


def per_device(matrix, column_weight, row_weight):
    n_rows = matrix.shape[0] * matrix.shape[2]
    dma = pltpu.SemaphoreType.DMA
    outs = [
        ((n_rows, 128), F32), ((256, 512), BF16), ((128, 512), BF16), ((8, 256), F32),
        ((4, 64, 128), F32), ((32, 128), F32), ((8, 128), F32),
    ]
    vmem = pl.BlockSpec(memory_space=pltpu.VMEM)
    got = pl.pallas_call(
        exchange,
        out_shape=[jax.ShapeDtypeStruct(*s) for s in outs],
        in_specs=[pl.BlockSpec(memory_space=pltpu.HBM)] * 3,
        out_specs=[vmem] * len(outs),
        scratch_shapes=[
            pltpu.VMEM((4, 128, 128), F32),
            pltpu.VMEM((136, 128), F32),
            pltpu.VMEM((128, 128), F32),
            pltpu.VMEM((128, 128), F32),
            pltpu.VMEM((2, 8, 128), F32),
            pltpu.VMEM((128, 128), F32),
            pltpu.VMEM((128, 128), F32),
            pltpu.VMEM((4, n_rows, 128), F32),
            pltpu.VMEM((4, 128), F32),
            pltpu.VMEM((32, 64), F32),
            pltpu.VMEM((3, 8, 128), F32),
            pltpu.VMEM((8, 8, 128), F32),
            pltpu.VMEM((32, 128), F32),
            pltpu.VMEM((8, 8, 128), F32),
            dma((6,)), dma((14,)), dma((4,)),
            dma((CH,)), dma((CH,)), dma((CH,)), dma((CH,)),
            dma((CH,)), dma((CH,)), dma((CH,)), dma((CH,)), dma((CH,)), dma((3 * CH,)),
            dma((3,)), dma((3,)), dma((7,)), dma((7,)), dma((3,)), dma((3,)),
            dma((7,)), dma((2,)), dma((7,)), dma((7,)), dma((9,)), dma((1,)),
            dma((9,)), dma((1,)),
        ]
        + [pltpu.SemaphoreType.REGULAR] * 4,
        compiler_params=pltpu.CompilerParams(
            collective_id=0, has_side_effects=True, vmem_limit_bytes=24 << 20
        ),
        name="exchange",
    )(
        in_hbm(matrix.reshape(n_rows, 4, 128)),
        in_hbm(column_weight.reshape(4, 128)),
        in_hbm(row_weight.reshape(32, 64)),
    )
    rows = n_rows // STEPS
    whole = lambda s: pl.BlockSpec(s, lambda i: (0,) * len(s))
    out, r, c = pl.pallas_call(
        update,
        grid=(STEPS,),
        out_shape=[
            jax.ShapeDtypeStruct((n_rows * 4, 128), F32),
            jax.ShapeDtypeStruct((32, 64), F32),
            jax.ShapeDtypeStruct((4, 128), F32),
        ],
        in_specs=[
            pl.BlockSpec((rows * 4, 128), lambda i: (i, 0)),
            pl.BlockSpec((rows, 128), lambda i: (i, 0)),
        ]
        + [whole(s) for s, _ in outs[1:]],
        out_specs=[
            pl.BlockSpec((rows * 4, 128), lambda i: (i, 0)),
            whole((32, 64)),
            whole((4, 128)),
        ],
        compiler_params=pltpu.CompilerParams(vmem_limit_bytes=24 << 20),
        name="update",
    )(matrix.reshape(n_rows * 4, 128), *got)
    return (
        out.reshape(matrix.shape),
        r.reshape(row_weight.shape),
        c.reshape(column_weight.shape),
    )


def solution(mesh):
    return jax.shard_map(
        per_device,
        mesh=mesh,
        in_specs=(
            P(None, "col", None, None, "row", None),
            P(None, "row", None),
            P(None, "col", None),
        ),
        out_specs=(
            P(None, "col", None, None, "row", None),
            P(None, "col", None),
            P(None, "row", None),
        ),
        check_vma=False,
    )
```

time: 49.6 us -> 43.1 us (0.87)
  the two profiles are of different devices: /device:TPU:155 before, /device:TPU:135 now
where the time goes in v3:
time: 43.1 us; the launch traced here: 42.3 us
  Pallas kernels  41.7 us (97%)
  between operations  0.65 us (2%)
    pallas_call x1, Pallas kernels, per_device(): pl.pallas_call(exchange, out_shape=[jax.ShapeDtypeStruct(*s) for s in out...  36.7 us
    pallas_call x1, Pallas kernels, per_device(): pl.pallas_call(update, grid=(STEPS,), out_shape=[jax.ShapeDtypeStruct((n_...  5.02 us

profile of v3, /device:TPU:135, one launch (start us, length us, event | category | flops | bytes accessed | tf_op | source)
XLA Modules:
  0.0 42.3 jit_solution(9041000740402147741)
XLA Ops:
  0.6 0.0 copy-start
  0.6 36.7 %exchange.1 = (f32[2048,128]{1,0:T(8,128)S(1)}, bf16[256,512]{1,0:T(8,128)(2,1)S(1)}, bf16[128,512]{1,0:T(8,128)(2,1)S(1)}, f32[8,256]{1,0:T(8,128)S(1)}, f32[4,...) custom-call(f32[2048,4,128]{2,1,0:T(4,128)} %bitcast.13, f32[4,128]{1,0:T(4,128)} %bitcast.16, ...), custom_call_target="tpu_custom_call" | custom-call | tf_op jit(solution)/shard_map/exchange/pallas_call | solution.py:679
  37.3 0.0 copy-done
  37.3 5.0 %update.1 = (f32[8192,128]{1,0:T(8,128)}, f32[32,64]{1,0:T(8,128)}, f32[4,128]{1,0:T(4,128)}) custom-call(f32[8192,128]{1,0:T(8,128)S(1)} %bitcast.14, f32[2048,128]{1,0:T(8,128)S(1)} %get-tuple-element.13.p_ref, bf16[256,512]{1,0:T(8,128)(2,1)S(1)} %get-tuple-element.14.xx_ref, bf16[128,512]{1,0:T(8,128)(2,1)S(1)} %get-tuple-element.15.xl_ref, ...), custom_call_target="tpu_custom_call" | custom-call | tf_op jit(solution)/shard_map/update/pallas_call | solution.py:718
Async XLA Ops:
  0.6 36.7 %copy-start = (f32[32,1,64,4,1,128]{5,4,3,2,1,0:T(1,128)S(1)}, f32[32,1,64,4,1,128]{5,4,3,2,1,0:T(1,128)}, u32[]{:S(2)}) copy-start(f32[32,1,64,4,1,128]{5,4,3,2,1,0:T(1,128)} %param.3) | copy-start | bytes 12582916

commit v4 on v3

--- a/solution.py
+++ b/solution.py
@@ -6,12 +6,13 @@
 from jax.sharding import PartitionSpec as P
 
 MESH = pl.DeviceIdType.MESH
-highest = lax.Precision.HIGHEST
+highest = lax.Precision.HIGH
 F32 = jnp.float32
 BF16 = jnp.bfloat16
 NZ = 8
 CH = 8
-STEPS = 8
+PART = 512 // CH
+STEPS = 2
 
 
 def dot(a, b):
@@ -85,11 +86,11 @@
     a_hbm, w_hbm, v_hbm,
     p_ref, xx_ref, xl_ref, xr_ref, u_ref, r_ref, c_ref,
     t_ref, inv_ref, rows_ref, low_ref, rk_ref,
-    cols_ref, diag_ref, a_ref, w_ref, v_ref, rq_ref, rz_ref, rs_ref, cz_ref,
+    cols_ref, diag_ref, a_ref, w_ref, v_ref, rq_ref, rz_ref, rs_ref, cz_ref, kq_ref, kz_ref,
     load_sem, t_send, t_recv, own_recv, sib_recv, y_recv, rel_recv,
     dn_send, dn2_send, sib_send, y_send, rel_send, root_send,
     rq_send, rq_recv, rz_send, rz_recv, rg_send, rg_recv, rk_send, rk_recv,
-    c_send, c_recv, i_send, i_recv, l_send, l_recv,
+    c_send, c_recv, i_send, i_recv, l_send, l_recv, kq_send, kq_recv, kz_send, kz_recv,
     dn_ready, dn2_ready, z_ready, z_go,
 ):
     me = lax.axis_index("row")
@@ -128,6 +129,11 @@
     loads.append(pltpu.make_async_copy(v_hbm, v_ref, load_sem.at[5]))
     for x in loads:
         x.start()
+    panel_load = pltpu.make_async_copy(a_hbm.at[:, 0, :], p_ref, load_sem.at[6])
+
+    @pl.when(is_root)
+    def _():
+        panel_load.start()
 
     barrier = pltpu.get_barrier_semaphore()
     for x in q_peers + c_peers:
@@ -142,8 +148,43 @@
     def _():
         signal(barrier, dn_to)
 
+    pl.semaphore_wait(
+        barrier, 10 + jnp.where(at_zero, 0, 1) + jnp.where(jnp.logical_and(z > 1, z < 7), 1, 0)
+    )
+
+    @pl.when(off_zero)
+    def _():
+        @pl.when(z == 7)
+        def _():
+            signal(dn2_ready, up_from)
+
+        @pl.when(z != 7)
+        def _():
+            signal(dn_ready, up_from)
+
+        signal(z_ready, at_row(q))
+
     for x in loads:
         x.wait()
+
+    @pl.when(heads)
+    def _():
+        mine = pl.ds(pl.multiple_of(col * 64, 64), 64)
+        t_ref[:, mine, :] = a_ref[:, 0:64, :]
+
+    def t_copy(part, i, src):
+        blocks = pl.ds(0, 1) if part == 0 else pl.ds(1, 3)
+        mine = pl.ds(pl.multiple_of(src * 64, 64), 64)
+        return pltpu.make_async_remote_copy(
+            t_ref.at[blocks, mine, :], t_ref.at[blocks, mine, :],
+            t_send.at[part * 7 + i], t_recv.at[part * 2 + src],
+            device_id=c_peers[i], device_id_type=MESH,
+        )
+
+    @pl.when(heads)
+    def _():
+        for i in range(7):
+            t_copy(0, i, col).start()
 
     def sums(t, acc):
         at = pl.multiple_of(t * 64, 64)
@@ -165,47 +206,61 @@
         c_ref[b : b + 1, :] = jnp.sum(acc[b], axis=0, keepdims=True)
     c_ref[4:8, :] = jnp.zeros((4, 128), F32)
 
-    @pl.when(is_root)
-    def _():
-        p_ref[...] = a_ref[0]
-
-    pl.semaphore_wait(
-        barrier, 10 + jnp.where(at_zero, 0, 1) + jnp.where(jnp.logical_and(z > 1, z < 7), 1, 0)
-    )
-
-    @pl.when(off_zero)
-    def _():
-        @pl.when(z == 7)
-        def _():
-            signal(dn2_ready, up_from)
-
-        @pl.when(z != 7)
-        def _():
-            signal(dn_ready, up_from)
-
-        signal(z_ready, at_row(q))
+    cz_ref[pl.ds(col, 1)] = c_ref[...][None]
+
+    def c_copy(i):
+        return pltpu.make_async_remote_copy(
+            cz_ref.at[col], cz_ref.at[col], c_send.at[i], c_recv.at[i],
+            device_id=c_peers[i], device_id_type=MESH,
+        )
+
+    for i in range(7):
+        c_copy(i).start()
+
+    def rq_copy(i):
+        to = lax.rem(q + i + 1, 4)
+        return pltpu.make_async_remote_copy(
+            r_ref.at[pl.ds(pl.multiple_of(to * 8, 8), 8)], rq_ref.at[i],
+            rq_send.at[i], rq_recv.at[i],
+            device_id=q_peers[i], device_id_type=MESH,
+        )
+
+    for i in range(3):
+        rq_copy(i).start()
+
+    kq_ref[pl.ds(q, 1)] = r_ref[0:8, :][None]
+
+    def kq_copy(i):
+        return pltpu.make_async_remote_copy(
+            kq_ref.at[q], kq_ref.at[q], kq_send.at[i], kq_recv.at[i],
+            device_id=q_peers[i], device_id_type=MESH,
+        )
+
+    def kz_copy(i):
+        return pltpu.make_async_remote_copy(
+            kz_ref.at[z], kz_ref.at[z], kz_send.at[i], kz_recv.at[i],
+            device_id=z_peers[i], device_id_type=MESH,
+        )
+
+    def kq_arrival(i):
+        return pltpu.make_async_remote_copy(
+            kq_ref.at[q], kq_ref.at[lax.rem(q + 3 - i, 4)], kq_send.at[i], kq_recv.at[i],
+            device_id=q_peers[i], device_id_type=MESH,
+        )
+
+    def kz_arrival(i):
+        return pltpu.make_async_remote_copy(
+            kz_ref.at[z], kz_ref.at[lax.rem(z + NZ - 1 - i, NZ)], kz_send.at[i], kz_recv.at[i],
+            device_id=z_peers[i], device_id_type=MESH,
+        )
 
     @pl.when(heads)
     def _():
-        mine = pl.ds(pl.multiple_of(col * 64, 64), 64)
-        t_ref[:, mine, :] = a_ref[:, 0:64, :]
-
-    def t_copy(part, i, src):
-        blocks = pl.ds(0, 1) if part == 0 else pl.ds(1, 3)
-        mine = pl.ds(pl.multiple_of(src * 64, 64), 64)
-        return pltpu.make_async_remote_copy(
-            t_ref.at[blocks, mine, :], t_ref.at[blocks, mine, :],
-            t_send.at[part * 7 + i], t_recv.at[part * 2 + src],
-            device_id=c_peers[i], device_id_type=MESH,
-        )
-
-    @pl.when(heads)
-    def _():
-        for i in range(7):
-            t_copy(0, i, col).start()
+        for i in range(3):
+            kq_copy(i).start()
 
     def piece(n, k):
-        return pl.ds(pl.multiple_of(n * (CH * 64) + k * 64, 64), 64)
+        return pl.ds(pl.multiple_of(n * 512 + k * PART, PART), PART)
 
     def p_copy(n, k, send, recv, to):
         return pltpu.make_async_remote_copy(
@@ -243,45 +298,19 @@
 
     @pl.when(is_root)
     def _():
+        panel_load.wait()
+
+    @pl.when(at_zero)
+    def _():
+        pl.semaphore_wait(dn_ready, 1)
+
+    @pl.when(is_root)
+    def _():
         def out(k, _):
-            for n in (2, 3, 1):
-                root_copy(n, k).start()
-            return 0
-
-        lax.fori_loop(0, CH, out, 0)
-
-    cz_ref[pl.ds(col, 1)] = c_ref[...][None]
-
-    def c_copy(i):
-        return pltpu.make_async_remote_copy(
-            cz_ref.at[col], cz_ref.at[col], c_send.at[i], c_recv.at[i],
-            device_id=c_peers[i], device_id_type=MESH,
-        )
-
-    for i in range(7):
-        c_copy(i).start()
-
-    def rq_copy(i):
-        to = lax.rem(q + i + 1, 4)
-        return pltpu.make_async_remote_copy(
-            r_ref.at[pl.ds(pl.multiple_of(to * 8, 8), 8)], rq_ref.at[i],
-            rq_send.at[i], rq_recv.at[i],
-            device_id=q_peers[i], device_id_type=MESH,
-        )
-
-    for i in range(3):
-        rq_copy(i).start()
-
-    @pl.when(at_zero)
-    def _():
-        pl.semaphore_wait(dn_ready, 1)
-
-    @pl.when(is_root)
-    def _():
-        def out(k, _):
+            root_copy(2, k).start()
             p_copy(q, k, dn_send, own_recv, dn_to).start()
-            pass_quad(k)
-            pass_opp(k)
+            root_copy(3, k).start()
+            root_copy(1, k).start()
             return 0
 
         lax.fori_loop(0, CH, out, 0)
@@ -306,6 +335,15 @@
         )
 
     def spread_quarter():
+        @pl.when(heads)
+        def _():
+            for i in range(3):
+                kq_copy(i).wait_send()
+                kq_arrival(i).wait_recv()
+            kz_ref[pl.ds(z, 1)] = (kq_ref[0] + kq_ref[1] + kq_ref[2] + kq_ref[3])[None]
+            for i in range(7):
+                kz_copy(i).start()
+
         for i in range(3):
             rq_copy(i).wait()
         total = r_ref[quarter, :] + rq_ref[0] + rq_ref[1] + rq_ref[2]
@@ -326,7 +364,24 @@
             device_id=q_peers[i], device_id_type=MESH,
         )
 
+    def rk_copy(i):
+        return pltpu.make_async_remote_copy(
+            rk_ref.at[col], rk_ref.at[col], rk_send.at[i], rk_recv.at[col],
+            device_id=c_peers[i], device_id_type=MESH,
+        )
+
     def gather_quarters():
+        @pl.when(heads)
+        def _():
+            for i in range(7):
+                kz_arrival(i).wait_recv()
+            top = kz_ref[0]
+            for i in range(1, 8):
+                top = top + kz_ref[i]
+            rk_ref[pl.ds(col, 1)] = top[None]
+            for i in range(7):
+                rk_copy(i).start()
+
         for i in range(7):
             rz_arrival(i).wait_recv()
         whole = rz_ref[0]
@@ -336,22 +391,6 @@
         for i in range(3):
             rg_copy(i).start()
 
-    def rk_copy(i):
-        return pltpu.make_async_remote_copy(
-            rs_ref.at[pl.ds(0, 8)], rk_ref.at[col], rk_send.at[i], rk_recv.at[col],
-            device_id=c_peers[i], device_id_type=MESH,
-        )
-
-    def spread_pivot_checks():
-        for i in range(3):
-            rg_arrival(i).wait_recv()
-
-        @pl.when(heads)
-        def _():
-            rk_ref[pl.ds(col, 1)] = rs_ref[0:8, :][None]
-            for i in range(7):
-                rk_copy(i).start()
-
     def take_own(k, _):
         p_copy(q, k, dn_send, own_recv, dn_to).wait_recv()
 
@@ -399,7 +438,7 @@
 
     even = lax.rem(q, 2) == 0
     over_z = jnp.logical_and(at_zero, even)
-    z_order = (3, 4, 2, 5, 1, 0, 6)
+    z_order = (0, 6, 1, 5, 2, 4, 3)
 
     def take_inverse():
         i_copy(0, sib).wait_recv()
@@ -428,7 +467,7 @@
 
     @pl.when(jnp.logical_and(at_zero, not_root))
     def _():
-        own(0, 4)
+        own(0, 2)
 
     @pl.when(at_zero)
     def _():
@@ -441,6 +480,13 @@
     def _():
         lax.fori_loop(0, CH, pass_dn2, 0)
         spread_quarter()
+
+        def rest(k, _):
+            pass_quad(k)
+            pass_opp(k)
+            return 0
+
+        lax.fori_loop(0, CH, rest, 0)
         for s in range(2):
             @pl.when(col != s)
             def _():
@@ -456,24 +502,24 @@
         i1 = lax.broadcasted_iota(jnp.int32, (128, 128), 1)
         inner = diag_ref[...] + jnp.where(i0 == i1, 1.0, 0.0)
         low_ref[...] = jnp.where(i0 // 8 > i1 // 8, -dot(cols_ref[...], inner), inner)
-        spread_pivot_checks()
 
     @pl.when(jnp.logical_and(at_zero, not_root))
     def _():
-        lax.fori_loop(0, 4, pass_dn2, 0)
+        lax.fori_loop(0, 2, pass_dn2, 0)
         spread_quarter()
 
         def both(k, _):
             take_own(k, 0)
             return pass_dn2(k, 0)
 
-        lax.fori_loop(4, CH, both, 0)
+        lax.fori_loop(2, CH, both, 0)
+        gather_quarters()
         lax.fori_loop(0, CH, take_opp, 0)
-        gather_quarters()
         take_inverse()
-        spread_pivot_checks()
-
-    near = jnp.logical_or(z == 1, z == 7)
+
+    away = jnp.where(z <= 4, z, NZ - z)
+    early = jnp.where(away <= 1, CH, jnp.where(away == 2, CH // 2, 0))
+    before = jnp.where(away <= 1, CH, 0)
 
     @pl.when(off_zero)
     def _():
@@ -484,22 +530,12 @@
 
         spread_quarter()
 
-        @pl.when(near)
-        def _():
-            own(0, CH)
-            gather_quarters()
-            lax.fori_loop(0, CH, take_opp, 0)
-            spread_pivot_checks()
-            take_inverse()
-
-        @pl.when(jnp.logical_not(near))
-        def _():
-            gather_quarters()
-            own(0, 4)
-            spread_pivot_checks()
-            own(4, CH)
-            take_inverse()
-            lax.fori_loop(0, CH, take_opp, 0)
+        own(0, early)
+        gather_quarters()
+        own(early, CH)
+        lax.fori_loop(0, before, take_opp, 0)
+        take_inverse()
+        lax.fori_loop(before, CH, take_opp, 0)
 
     @pl.when(not_root)
     def _():
@@ -514,7 +550,7 @@
 
             t_copy(1, 0, s).wait_recv()
             pltpu.make_async_remote_copy(
-                rs_ref.at[pl.ds(0, 8)], rk_ref.at[s], rk_send.at[0], rk_recv.at[s],
+                rk_ref.at[s], rk_ref.at[s], rk_send.at[0], rk_recv.at[s],
                 device_id=c_peers[0], device_id_type=MESH,
             ).wait_recv()
 
@@ -544,6 +580,8 @@
     rk = jnp.concatenate([rk_ref[0, :, 0:64], rk_ref[1, :, 0:64]], axis=1)
     rk = jnp.broadcast_to(rk[0:1, :], (8, 128))
     xr_ref[:, 0:128] = dot_t(rk, inv)
+    for i in range(3):
+        rg_arrival(i).wait_recv()
     r_ref[...] = rs_ref[...]
 
     @pl.when(heads)
@@ -576,6 +614,7 @@
             t_copy(0, i, col).wait_send()
             t_copy(1, i, col).wait_send()
             rk_copy(i).wait_send()
+            kz_copy(i).wait_send()
 
     for i in range(7):
         c_copy(i).wait_send()
@@ -696,12 +735,14 @@
             pltpu.VMEM((8, 8, 128), F32),
             pltpu.VMEM((32, 128), F32),
             pltpu.VMEM((8, 8, 128), F32),
-            dma((6,)), dma((14,)), dma((4,)),
+            pltpu.VMEM((4, 8, 128), F32),
+            pltpu.VMEM((8, 8, 128), F32),
+            dma((7,)), dma((14,)), dma((4,)),
             dma((CH,)), dma((CH,)), dma((CH,)), dma((CH,)),
             dma((CH,)), dma((CH,)), dma((CH,)), dma((CH,)), dma((CH,)), dma((3 * CH,)),
             dma((3,)), dma((3,)), dma((7,)), dma((7,)), dma((3,)), dma((3,)),
             dma((7,)), dma((2,)), dma((7,)), dma((7,)), dma((9,)), dma((1,)),
-            dma((9,)), dma((1,)),
+            dma((9,)), dma((1,)), dma((3,)), dma((3,)), dma((7,)), dma((7,)),
         ]
         + [pltpu.SemaphoreType.REGULAR] * 4,
         compiler_params=pltpu.CompilerParams(

time: 43.1 us -> 38.5 us (0.89); the launches traced: 42.3 us -> 38.4 us
  Pallas kernels: 41.7 us -> 37.8 us
    pallas_call x1, Pallas kernels: 36.7 us -> 34.7 us  [per_device(): pl.pallas_call(exchange, out_shape=[jax.ShapeDtypeStruct(*s) for s in out...]
    pallas_call x1, Pallas kernels: 5.02 us -> 3.1 us  [per_device(): pl.pallas_call(update, grid=(STEPS,), out_shape=[jax.ShapeDtypeStruct((n_...]
where the time goes in v4:
time: 38.5 us; the launch traced here: 38.4 us
  Pallas kernels  37.8 us (98%)
  between operations  0.65 us (2%)
    pallas_call x1, Pallas kernels, per_device(): pl.pallas_call(exchange, out_shape=[jax.ShapeDtypeStruct(*s) for s in out...  34.7 us
    pallas_call x1, Pallas kernels, per_device(): pl.pallas_call(update, grid=(STEPS,), out_shape=[jax.ShapeDtypeStruct((n_...  3.1 us

profile of v4, /device:TPU:135, one launch (start us, length us, event | category | flops | bytes accessed | tf_op | source)
XLA Modules:
  0.0 38.4 jit_solution(11170568766441785605)
XLA Ops:
  0.6 0.0 copy-start
  0.6 34.7 %exchange.1 = (f32[2048,128]{1,0:T(8,128)S(1)}, bf16[256,512]{1,0:T(8,128)(2,1)S(1)}, bf16[128,512]{1,0:T(8,128)(2,1)S(1)}, f32[8,256]{1,0:T(8,128)S(1)}, f32[4,...) custom-call(f32[2048,4,128]{2,1,0:T(4,128)} %bitcast.13, f32[4,128]{1,0:T(4,128)} %bitcast.16, ...), custom_call_target="tpu_custom_call" | custom-call | tf_op jit(solution)/shard_map/exchange/pallas_call | solution.py:718
  35.3 0.0 copy-done
  35.3 3.1 %update.1 = (f32[8192,128]{1,0:T(8,128)}, f32[32,64]{1,0:T(8,128)}, f32[4,128]{1,0:T(4,128)}) custom-call(f32[8192,128]{1,0:T(8,128)S(1)} %bitcast.14, f32[2048,128]{1,0:T(8,128)S(1)} %get-tuple-element.13.p_ref, bf16[256,512]{1,0:T(8,128)(2,1)S(1)} %get-tuple-element.14.xx_ref, bf16[128,512]{1,0:T(8,128)(2,1)S(1)} %get-tuple-element.15.xl_ref, ...), custom_call_target="tpu_custom_call" | custom-call | tf_op jit(solution)/shard_map/update/pallas_call | solution.py:759
Async XLA Ops:
  0.6 34.7 %copy-start = (f32[32,1,64,4,1,128]{5,4,3,2,1,0:T(1,128)S(1)}, f32[32,1,64,4,1,128]{5,4,3,2,1,0:T(1,128)}, u32[]{:S(2)}) copy-start(f32[32,1,64,4,1,128]{5,4,3,2,1,0:T(1,128)} %param.3) | copy-start | bytes 12582916

commit v5 on v4

--- a/solution.py
+++ b/solution.py
@@ -10,8 +10,10 @@
 F32 = jnp.float32
 BF16 = jnp.bfloat16
 NZ = 8
-CH = 8
-PART = 512 // CH
+PART = 64
+LONG = 10
+SHORT = 6
+HEADSTART = 4
 STEPS = 2
 
 
@@ -186,6 +188,65 @@
         for i in range(7):
             t_copy(0, i, col).start()
 
+    def piece(n, k):
+        first = jnp.where(n < 2, n * LONG, 2 * LONG + (n - 2) * SHORT)
+        return pl.ds(pl.multiple_of((first + k) * PART, PART), PART)
+
+    def p_copy(n, k, send, recv, to):
+        return pltpu.make_async_remote_copy(
+            p_ref.at[piece(n, k)], p_ref.at[piece(n, k)],
+            send.at[k], recv.at[k], device_id=to, device_id_type=MESH,
+        )
+
+    mine_n = jnp.where(q < 2, LONG, SHORT)
+    opp_count = LONG + SHORT - mine_n
+    to_sib = jnp.logical_not(jnp.logical_and(at_zero, q == 1))
+    to_opp = jnp.logical_not(jnp.logical_and(at_zero, q == 2))
+
+    def pass_dn2(k, _):
+        p_copy(q, k, dn2_send, own_recv, dn2_to).start()
+        return 0
+
+    def pass_quad(k):
+        @pl.when(to_opp)
+        def _():
+            p_copy(q, k, y_send, y_recv, opp).start()
+
+        @pl.when(to_sib)
+        def _():
+            p_copy(q, k, sib_send, sib_recv, sib).start()
+
+    def pass_opp(k):
+        @pl.when(to_sib)
+        def _():
+            p_copy(opp_n, k, rel_send, rel_recv, sib).start()
+
+    def root_copy(n, k):
+        return pltpu.make_async_remote_copy(
+            p_ref.at[piece(n, k)], p_ref.at[piece(n, k)],
+            root_send.at[(n - 1) * LONG + k], own_recv.at[k],
+            device_id=at_row(n), device_id_type=MESH,
+        )
+
+    def send_two(k, _):
+        p_copy(q, k, dn_send, own_recv, dn_to).start()
+        root_copy(1, k).start()
+        return 0
+
+    def send_four(k, _):
+        root_copy(2, k).start()
+        root_copy(3, k).start()
+        return send_two(k, 0)
+
+    @pl.when(at_zero)
+    def _():
+        pl.semaphore_wait(dn_ready, 1)
+
+    @pl.when(is_root)
+    def _():
+        panel_load.wait()
+        lax.fori_loop(0, HEADSTART, send_four, 0)
+
     def sums(t, acc):
         at = pl.multiple_of(t * 64, 64)
         v = jnp.broadcast_to(v_ref[pl.ds(t, 1), :], (128, 64)).T
@@ -259,61 +320,10 @@
         for i in range(3):
             kq_copy(i).start()
 
-    def piece(n, k):
-        return pl.ds(pl.multiple_of(n * 512 + k * PART, PART), PART)
-
-    def p_copy(n, k, send, recv, to):
-        return pltpu.make_async_remote_copy(
-            p_ref.at[piece(n, k)], p_ref.at[piece(n, k)],
-            send.at[k], recv.at[k], device_id=to, device_id_type=MESH,
-        )
-
-    to_sib = jnp.logical_not(jnp.logical_and(at_zero, q == 1))
-    to_opp = jnp.logical_not(jnp.logical_and(at_zero, q == 2))
-
-    def pass_dn2(k, _):
-        p_copy(q, k, dn2_send, own_recv, dn2_to).start()
-        return 0
-
-    def pass_quad(k):
-        @pl.when(to_opp)
-        def _():
-            p_copy(q, k, y_send, y_recv, opp).start()
-
-        @pl.when(to_sib)
-        def _():
-            p_copy(q, k, sib_send, sib_recv, sib).start()
-
-    def pass_opp(k):
-        @pl.when(to_sib)
-        def _():
-            p_copy(opp_n, k, rel_send, rel_recv, sib).start()
-
-    def root_copy(n, k):
-        return pltpu.make_async_remote_copy(
-            p_ref.at[piece(n, k)], p_ref.at[piece(n, k)],
-            root_send.at[(n - 1) * CH + k], own_recv.at[k],
-            device_id=at_row(n), device_id_type=MESH,
-        )
-
     @pl.when(is_root)
     def _():
-        panel_load.wait()
-
-    @pl.when(at_zero)
-    def _():
-        pl.semaphore_wait(dn_ready, 1)
-
-    @pl.when(is_root)
-    def _():
-        def out(k, _):
-            root_copy(2, k).start()
-            p_copy(q, k, dn_send, own_recv, dn_to).start()
-            root_copy(3, k).start()
-            root_copy(1, k).start()
-            return 0
-
-        lax.fori_loop(0, CH, out, 0)
+        lax.fori_loop(HEADSTART, SHORT, send_four, 0)
+        lax.fori_loop(SHORT, LONG, send_two, 0)
 
     @pl.when(heads)
     def _():
@@ -478,15 +488,17 @@
 
     @pl.when(is_root)
     def _():
-        lax.fori_loop(0, CH, pass_dn2, 0)
+        lax.fori_loop(0, LONG, pass_dn2, 0)
         spread_quarter()
 
         def rest(k, _):
             pass_quad(k)
+            return 0
+
+        def rest_opp(k, _):
             pass_opp(k)
             return 0
 
-        lax.fori_loop(0, CH, rest, 0)
         for s in range(2):
             @pl.when(col != s)
             def _():
@@ -497,6 +509,8 @@
         for i in z_order:
             inv_to(i, z_peers[i])
         inv_to(8, sib)
+        lax.fori_loop(0, LONG, rest, 0)
+        lax.fori_loop(0, SHORT, rest_opp, 0)
         gather_quarters()
         i0 = lax.broadcasted_iota(jnp.int32, (128, 128), 0)
         i1 = lax.broadcasted_iota(jnp.int32, (128, 128), 1)
@@ -512,14 +526,14 @@
             take_own(k, 0)
             return pass_dn2(k, 0)
 
-        lax.fori_loop(2, CH, both, 0)
+        lax.fori_loop(2, mine_n, both, 0)
         gather_quarters()
-        lax.fori_loop(0, CH, take_opp, 0)
         take_inverse()
+        lax.fori_loop(0, opp_count, take_opp, 0)
 
     away = jnp.where(z <= 4, z, NZ - z)
-    early = jnp.where(away <= 1, CH, jnp.where(away == 2, CH // 2, 0))
-    before = jnp.where(away <= 1, CH, 0)
+    early = mine_n
+    before = jnp.where(away <= 1, opp_count, 0)
 
     @pl.when(off_zero)
     def _():
@@ -532,10 +546,10 @@
 
         own(0, early)
         gather_quarters()
-        own(early, CH)
+        own(early, mine_n)
         lax.fori_loop(0, before, take_opp, 0)
         take_inverse()
-        lax.fori_loop(before, CH, take_opp, 0)
+        lax.fori_loop(before, opp_count, take_opp, 0)
 
     @pl.when(not_root)
     def _():
@@ -601,12 +615,16 @@
 
     @pl.when(not_root)
     def _():
-        def body(k, _):
+        def from_sib(k, _):
             p_copy(sib_n, k, sib_send, sib_recv, sib).wait_recv()
+            return 0
+
+        def from_rel(k, _):
             p_copy(lax.rem(sib_n + 2, 4), k, rel_send, rel_recv, sib).wait_recv()
             return 0
 
-        lax.fori_loop(0, CH, body, 0)
+        lax.fori_loop(0, mine_n, from_sib, 0)
+        lax.fori_loop(0, opp_count, from_rel, 0)
 
     @pl.when(heads)
     def _():
@@ -638,16 +656,32 @@
         @pl.when(to_sib)
         def _():
             p_copy(q, k, sib_send, sib_recv, sib).wait_send()
-            p_copy(opp_n, k, rel_send, rel_recv, sib).wait_send()
-
-        @pl.when(is_root)
-        def _():
-            for n in (1, 2, 3):
-                root_copy(n, k).wait_send()
 
         return 0
 
-    lax.fori_loop(0, CH, sent, 0)
+    def sent_opp(k, _):
+        p_copy(opp_n, k, rel_send, rel_recv, sib).wait_send()
+        return 0
+
+    lax.fori_loop(0, mine_n, sent, 0)
+
+    @pl.when(to_sib)
+    def _():
+        lax.fori_loop(0, opp_count, sent_opp, 0)
+
+    @pl.when(is_root)
+    def _():
+        def sent_root(k, _):
+            root_copy(1, k).wait_send()
+            return 0
+
+        def sent_roots(k, _):
+            root_copy(2, k).wait_send()
+            root_copy(3, k).wait_send()
+            return 0
+
+        lax.fori_loop(0, LONG, sent_root, 0)
+        lax.fori_loop(0, SHORT, sent_roots, 0)
 
     @pl.when(over_z)
     def _():
@@ -738,8 +772,8 @@
             pltpu.VMEM((4, 8, 128), F32),
             pltpu.VMEM((8, 8, 128), F32),
             dma((7,)), dma((14,)), dma((4,)),
-            dma((CH,)), dma((CH,)), dma((CH,)), dma((CH,)),
-            dma((CH,)), dma((CH,)), dma((CH,)), dma((CH,)), dma((CH,)), dma((3 * CH,)),
+            dma((LONG,)), dma((LONG,)), dma((LONG,)), dma((LONG,)),
+            dma((LONG,)), dma((LONG,)), dma((LONG,)), dma((LONG,)), dma((LONG,)), dma((3 * LONG,)),
             dma((3,)), dma((3,)), dma((7,)), dma((7,)), dma((3,)), dma((3,)),
             dma((7,)), dma((2,)), dma((7,)), dma((7,)), dma((9,)), dma((1,)),
             dma((9,)), dma((1,)), dma((3,)), dma((3,)), dma((7,)), dma((7,)),

time: 38.5 us -> 37.3 us (0.969); the launches traced: 38.4 us -> 36.6 us
  Pallas kernels: 37.8 us -> 35.9 us
    pallas_call x1, Pallas kernels: 34.7 us -> 32.8 us  [per_device(): pl.pallas_call(exchange, out_shape=[jax.ShapeDtypeStruct(*s) for s in out...]
where the time goes in v5:
time: 37.3 us; the launch traced here: 36.6 us
  Pallas kernels  35.9 us (96%)
  between operations  0.65 us (2%)
    pallas_call x1, Pallas kernels, per_device(): pl.pallas_call(exchange, out_shape=[jax.ShapeDtypeStruct(*s) for s in out...  32.8 us
    pallas_call x1, Pallas kernels, per_device(): pl.pallas_call(update, grid=(STEPS,), out_shape=[jax.ShapeDtypeStruct((n_...  3.1 us

profile of v5, /device:TPU:135, one launch (start us, length us, event | category | flops | bytes accessed | tf_op | source)
XLA Modules:
  0.0 36.6 jit_solution(13655630636851032986)
XLA Ops:
  0.6 0.0 copy-start
  0.6 32.8 %exchange.1 = (f32[2048,128]{1,0:T(8,128)S(1)}, bf16[256,512]{1,0:T(8,128)(2,1)S(1)}, bf16[128,512]{1,0:T(8,128)(2,1)S(1)}, f32[8,256]{1,0:T(8,128)S(1)}, f32[4,...) custom-call(f32[2048,4,128]{2,1,0:T(4,128)} %bitcast.13, f32[4,128]{1,0:T(4,128)} %bitcast.16, ...), custom_call_target="tpu_custom_call" | custom-call | tf_op jit(solution)/shard_map/exchange/pallas_call | solution.py:752
  33.5 0.0 copy-done
  33.5 3.1 %update.1 = (f32[8192,128]{1,0:T(8,128)}, f32[32,64]{1,0:T(8,128)}, f32[4,128]{1,0:T(4,128)}) custom-call(f32[8192,128]{1,0:T(8,128)S(1)} %bitcast.14, f32[2048,128]{1,0:T(8,128)S(1)} %get-tuple-element.13.p_ref, bf16[256,512]{1,0:T(8,128)(2,1)S(1)} %get-tuple-element.14.xx_ref, bf16[128,512]{1,0:T(8,128)(2,1)S(1)} %get-tuple-element.15.xl_ref, ...), custom_call_target="tpu_custom_call" | custom-call | tf_op jit(solution)/shard_map/update/pallas_call | solution.py:793
Async XLA Ops:
  0.6 32.9 %copy-start = (f32[32,1,64,4,1,128]{5,4,3,2,1,0:T(1,128)S(1)}, f32[32,1,64,4,1,128]{5,4,3,2,1,0:T(1,128)}, u32[]{:S(2)}) copy-start(f32[32,1,64,4,1,128]{5,4,3,2,1,0:T(1,128)} %param.3) | copy-start | bytes 12582916

commit v6 on v5

--- a/solution.py
+++ b/solution.py
@@ -477,7 +477,7 @@
 
     @pl.when(jnp.logical_and(at_zero, not_root))
     def _():
-        own(0, 2)
+        own(0, 1)
 
     @pl.when(at_zero)
     def _():
@@ -519,14 +519,14 @@
 
     @pl.when(jnp.logical_and(at_zero, not_root))
     def _():
-        lax.fori_loop(0, 2, pass_dn2, 0)
+        lax.fori_loop(0, 1, pass_dn2, 0)
         spread_quarter()
 
         def both(k, _):
             take_own(k, 0)
             return pass_dn2(k, 0)
 
-        lax.fori_loop(2, mine_n, both, 0)
+        lax.fori_loop(1, mine_n, both, 0)
         gather_quarters()
         take_inverse()
         lax.fori_loop(0, opp_count, take_opp, 0)

time: 37.3 us -> 37.6 us (level)
  no operation moved by 1% of the time
where the time goes in v6:
time: 37.6 us; the launch traced here: 36.9 us
  Pallas kernels  36.2 us (96%)
  between operations  0.65 us (2%)
    pallas_call x1, Pallas kernels, per_device(): pl.pallas_call(exchange, out_shape=[jax.ShapeDtypeStruct(*s) for s in out...  33.1 us
    pallas_call x1, Pallas kernels, per_device(): pl.pallas_call(update, grid=(STEPS,), out_shape=[jax.ShapeDtypeStruct((n_...  3.1 us

profile of v6, /device:TPU:135, one launch (start us, length us, event | category | flops | bytes accessed | tf_op | source)
XLA Modules:
  0.0 36.9 jit_solution(8229042312323581726)
XLA Ops:
  0.6 0.0 copy-start
  0.6 33.1 %exchange.1 = (f32[2048,128]{1,0:T(8,128)S(1)}, bf16[256,512]{1,0:T(8,128)(2,1)S(1)}, bf16[128,512]{1,0:T(8,128)(2,1)S(1)}, f32[8,256]{1,0:T(8,128)S(1)}, f32[4,...) custom-call(f32[2048,4,128]{2,1,0:T(4,128)} %bitcast.13, f32[4,128]{1,0:T(4,128)} %bitcast.16, ...), custom_call_target="tpu_custom_call" | custom-call | tf_op jit(solution)/shard_map/exchange/pallas_call | solution.py:752
  33.8 0.0 copy-done
  33.8 3.1 %update.1 = (f32[8192,128]{1,0:T(8,128)}, f32[32,64]{1,0:T(8,128)}, f32[4,128]{1,0:T(4,128)}) custom-call(f32[8192,128]{1,0:T(8,128)S(1)} %bitcast.14, f32[2048,128]{1,0:T(8,128)S(1)} %get-tuple-element.13.p_ref, bf16[256,512]{1,0:T(8,128)(2,1)S(1)} %get-tuple-element.14.xx_ref, bf16[128,512]{1,0:T(8,128)(2,1)S(1)} %get-tuple-element.15.xl_ref, ...), custom_call_target="tpu_custom_call" | custom-call | tf_op jit(solution)/shard_map/update/pallas_call | solution.py:793
Async XLA Ops:
  0.6 33.2 %copy-start = (f32[32,1,64,4,1,128]{5,4,3,2,1,0:T(1,128)S(1)}, f32[32,1,64,4,1,128]{5,4,3,2,1,0:T(1,128)}, u32[]{:S(2)}) copy-start(f32[32,1,64,4,1,128]{5,4,3,2,1,0:T(1,128)} %param.3) | copy-start | bytes 12582916
